TPU v7x, 32 devices: a whole 2x2x4 slice. The times are simulated.
32 devices in a mesh: group: 2 (over y), seq: 16 (over z, x, core).
Axes of the slice: x: 2, y: 2, z: 4, core: 2. Of those that a mesh axis runs over, the one named last changes fastest.
Arguments:
- inputs: bfloat16 [12544, 1024], P(('group', 'seq')), parts along dimension 0, may hold values from -6 to 6
- out_grad: bfloat16 [12544, 1024], P(('group', 'seq')), parts along dimension 0, may hold values from -6 to 6
- live_rows: int32 [256], P('group'), parts along dimension 0, may hold values from 1 to 7
- live_cols: int32 [256], P('group'), parts along dimension 0, may hold values from 1 to 7
- norm_gain: float32 [1024], replicated, may hold values from 0.25 to 1.75
- norm_bias: float32 [1024], replicated, may hold values from -3 to 3
- w_query: bfloat16 [1024, 1024], replicated
- w_key_value: bfloat16 [1024, 2048], replicated
- w_out: bfloat16 [1024, 1024], replicated, may hold values from -0.1875 to 0.1875
Outputs:
- block_output: bfloat16 [12544, 1024], P(('group', 'seq')), parts along dimension 0
- input_grad: bfloat16 [12544, 1024], P(('group', 'seq')), parts along dimension 0
There are 2 independent parts, one for each index of `group`. A program takes and returns all parts, laid end to end along the dimension named above; an argument that names none is the same for every part. Nothing has to cross between parts.
All inputs are finite; a program needn't handle non-finite values.
Results may differ from a plain program's by a relative error of at most 0.006.
The roundings to bfloat16 on the way count: a program that leaves them out, or rounds other values in their place, can miss the bound.
Values may be sent and summed in bfloat16 or wider, within the bound.
No kernel may reach another device: no remote copies, remote signals or barrier semaphores. Data moves between devices by JAX's collectives and lax.ppermute only.
A program may use at most 192 MiB of HBM per device.

v0:
```python
import functools

import jax
import jax.numpy as jnp
import numpy as np
from jax import lax
from jax.experimental import pallas as pl
from jax.experimental.pallas import tpu as pltpu
from jax.sharding import PartitionSpec as P

HEAD_DIM = 32
WT = 8
WH = 7
WW = 7
CELLS = WH * WW
HALF = WT // 2
EPSILON = 1e-05
GROUP_LANES = 128
HEADS_PER_GROUP = GROUP_LANES // HEAD_DIM
SLOTS = (64, 48)
ROWS = sum(SLOTS)
FIRST = 2 * SLOTS[0]
SECOND = 2 * SLOTS[1]
WINDOW_ROWS = FIRST + SECOND
PADDED_ROWS = 2 * GROUP_LANES
MASKED = -1e30
BF16 = jnp.bfloat16
F32 = jnp.float32
NT = (((1,), (1,)), ((), ()))


def quadrant_cells(quadrant):
    rows = range(WH // 2) if quadrant & 2 else range(WH // 2, WH)
    cols = range(WW // 2) if quadrant & 1 else range(WW // 2, WW)
    return [(row, col) for row in rows for col in cols]


def half_slots(units):
    slots = []
    for quadrant, room in zip(units, SLOTS):
        entries = [(frame, row, col) for frame in range(HALF) for row, col in quadrant_cells(quadrant)]
        slots += entries + [None] * (room - len(entries))
    return slots


def tables():
    takes = {"last": (0, 3), "first": (1, 2)}
    gives = {"last": (1, 2), "first": (0, 3)}

    def tokens(side, units):
        shift = HALF if side == "last" else 0
        return [-1 if s is None else (s[0] + shift) * CELLS + s[1] * WW + s[2] for s in half_slots(units)]

    def codes(slots, second_half):
        return [-1 if s is None else (s[0] + HALF * second_half) * 64 + s[1] * 8 + s[2] for s in slots]

    own, send, window = [], [], []
    for parity in range(2):
        sides = ("last", "first") if parity == 0 else ("first", "last")
        own.append(sum((tokens(side, takes[side]) for side in sides), []))
        send.append(sum((tokens(side, gives[side]) for side in sides), []))
    for side in ("first", "last"):
        slots = half_slots(takes[side])
        mine = codes(slots, side == "first")
        theirs = codes(slots, side == "last")
        cut = SLOTS[0]
        rows = mine[:cut] + theirs[:cut] + mine[cut:] + theirs[cut:]
        window.append(rows + [-1] * (PADDED_ROWS - len(rows)))
    return np.array(own, np.int32), np.array(send, np.int32), np.array(window, np.int32)


OWN_TOKENS, SEND_TOKENS, WINDOW_CODES = tables()


def normalized(values_in):
    values = values_in.astype(F32)
    centred = values - jnp.mean(values, axis=-1, keepdims=True)
    inv_dev = lax.rsqrt(jnp.mean(centred * centred, axis=-1, keepdims=True) + EPSILON)
    return centred * inv_dev, inv_dev


def one_hot_rows(token_column, token_count):
    lanes = lax.broadcasted_iota(jnp.int32, (token_column.shape[0], token_count), 1)
    return (lanes == token_column).astype(F32).astype(BF16)


def picked(one_hot, values):
    return jnp.dot(one_hot, values, preferred_element_type=F32).astype(BF16)


def pack_kernel(meta, table, inputs, out_grad, same, cross):
    width = inputs.shape[1]
    one_hot = one_hot_rows(table[meta[0]], inputs.shape[0])
    for place, source in enumerate((inputs, out_grad)):
        rows = picked(one_hot, source[...])
        columns = slice(place * width, (place + 1) * width)
        same[:, columns] = rows[:ROWS]
        cross[:, columns] = rows[ROWS:]


def project(values, grads, gain, bias, w_query, w_key_value, w_out, store):
    width = values.shape[1]
    unit, _ = normalized(values)
    hidden = (unit * gain[...] + bias[...]).astype(BF16)
    store(0, jnp.dot(hidden, w_query[...], preferred_element_type=F32).astype(BF16))
    store(width, jnp.dot(hidden, w_key_value[...], preferred_element_type=F32).astype(BF16))
    store(3 * width, lax.dot_general(grads, w_out[...], NT, preferred_element_type=F32).astype(BF16))


def own_kernel(
    meta, table, inputs, out_grad, gain, bias, w_query, w_key_value, w_out, rows_same, rows_cross, heads_same, heads_cross
):
    width = inputs.shape[1]
    one_hot = one_hot_rows(table[meta[0]], inputs.shape[0])
    values = picked(one_hot, inputs[...])
    grads = picked(one_hot, out_grad[...])
    for place, rows in enumerate((values, grads)):
        columns = slice(place * width, (place + 1) * width)
        rows_same[:, columns] = rows[:ROWS]
        rows_cross[:, columns] = rows[ROWS:]

    def store(column, result):
        columns = slice(column, column + result.shape[1])
        heads_same[:, columns] = result[:ROWS]
        heads_cross[:, columns] = result[ROWS:]

    project(values, grads, gain, bias, w_query, w_key_value, w_out, store)


def cell_codes(slots, place, frames):
    frame = slots >> 6
    word = jnp.zeros_like(slots)
    for index, frame_word in enumerate(frames):
        word = jnp.where(frame == index, frame_word, word)
    row, col = (slots >> 3) & 7, slots & 7
    live = (slots >= 0) & (row < (word >> 8)) & (col < ((word >> 4) & 15))
    return jnp.where(live, word & 1, -1 - place)


def attend(heads, results, bias_of, group, width):
    scale = HEAD_DIM ** (-0.5)
    lane = lax.broadcasted_iota(jnp.int32, (GROUP_LANES, GROUP_LANES), 1) // HEAD_DIM

    def columns(part):
        return pl.ds(pl.multiple_of(part * width + group * GROUP_LANES, GROUP_LANES), GROUP_LANES)

    for unit, count in enumerate((FIRST, SECOND)):
        base = unit * GROUP_LANES
        keys = slice(base, base + count)
        query = heads[base : base + GROUP_LANES, columns(0)]
        key = heads[keys, columns(1)]
        value = heads[keys, columns(2)]
        grad = heads[base : base + GROUP_LANES, columns(3)]
        zero = jnp.zeros_like(query)
        query_stack = jnp.concatenate([jnp.where(lane == h, query, zero) for h in range(HEADS_PER_GROUP)], axis=0)
        grad_stack = jnp.concatenate([jnp.where(lane == h, grad, zero) for h in range(HEADS_PER_GROUP)], axis=0)
        score = lax.dot_general(key, query_stack, NT, preferred_element_type=F32)
        grad_probs = lax.dot_general(value, grad_stack, NT, preferred_element_type=F32)
        bias = bias_of[keys, :]
        bias = jnp.concatenate([bias] * HEADS_PER_GROUP, axis=1)
        score = score * scale + bias
        raw = jnp.exp(score - jnp.max(score, axis=0, keepdims=True))
        probs = raw * (1.0 / jnp.sum(raw, axis=0, keepdims=True))
        row_dot = jnp.sum(probs * grad_probs, axis=0, keepdims=True)
        grad_score = (probs * (grad_probs - row_dot) * scale).astype(BF16)
        probs_low = probs.astype(BF16)
        grad_value = jnp.dot(probs_low, grad_stack, preferred_element_type=F32)
        grad_key = jnp.dot(grad_score, query_stack, preferred_element_type=F32)
        key_t, value_t = key.T, value.T

        def per_head(left, right):
            parts = []
            for h in range(HEADS_PER_GROUP):
                rows = slice(h * HEAD_DIM, (h + 1) * HEAD_DIM)
                lanes = slice(h * GROUP_LANES, (h + 1) * GROUP_LANES)
                parts.append(jnp.dot(left[rows], right[:, lanes], preferred_element_type=F32))
            return jnp.concatenate(parts, axis=0).T[:count].astype(BF16)

        results[keys, columns(0)] = per_head(value_t, probs_low)
        results[keys, columns(1)] = per_head(key_t, grad_score)
        results[keys, columns(2)] = grad_key.astype(BF16)
        results[keys, columns(3)] = grad_value.astype(BF16)


def finish(rows, results, gain, w_query, w_key_value, w_out):
    width = rows.shape[1] // 2
    values, grads = rows[:, :width], rows[:, width:]
    block_output = values.astype(F32) + jnp.dot(results[:, :width], w_out[...], preferred_element_type=F32)
    grad_hidden = lax.dot_general(results[:, width : 2 * width], w_query[...], NT, preferred_element_type=F32)
    grad_hidden = grad_hidden + lax.dot_general(
        results[:, 2 * width :], w_key_value[...], NT, preferred_element_type=F32
    )
    unit, inv_dev = normalized(values)
    scaled = grad_hidden * gain[...]
    centred = scaled - jnp.mean(scaled, axis=-1, keepdims=True)
    norm_grad = inv_dev * (centred - unit * jnp.mean(scaled * unit, axis=-1, keepdims=True))
    input_grad = grads.astype(F32) + norm_grad
    return jnp.concatenate([block_output.astype(BF16), input_grad.astype(BF16)], axis=1)


def window_kernel(
    kind, meta, code_column, code_row, own_rows, own_heads, far_rows, gain, bias, w_query, w_key_value, w_out,
    far_result, own_result, heads, results, bias_of
):
    width = far_rows.shape[1] // 2
    cut = SLOTS[0]
    side = 1 - meta[0] if kind == "same" else meta[0]
    frames = [meta[1 + side * WT + index] for index in range(WT)]
    place_column = lax.broadcasted_iota(jnp.int32, (PADDED_ROWS, 1), 0)
    place_row = lax.broadcasted_iota(jnp.int32, (1, PADDED_ROWS), 1)
    by_key = cell_codes(code_column[side], place_column, frames)
    by_query = cell_codes(code_row[side], place_row, frames)
    for unit in range(2):
        block = slice(unit * GROUP_LANES, (unit + 1) * GROUP_LANES)
        bias_of[block, :] = jnp.where(by_key[block] == by_query[:, block], 0.0, MASKED)

    heads[:cut] = own_heads[:cut]
    heads[FIRST : FIRST + SLOTS[1]] = own_heads[cut:]
    heads[WINDOW_ROWS:] = jnp.zeros((PADDED_ROWS - WINDOW_ROWS, heads.shape[1]), BF16)

    def store(column, result):
        columns = slice(column, column + result.shape[1])
        heads[cut:FIRST, columns] = result[:cut]
        heads[FIRST + SLOTS[1] : WINDOW_ROWS, columns] = result[cut:]

    project(far_rows[:, :width], far_rows[:, width:], gain, bias, w_query, w_key_value, w_out, store)

    def body(group, carry):
        attend(heads, results, bias_of, group, width)
        return carry

    lax.fori_loop(0, width // GROUP_LANES, body, 0)

    far = jnp.concatenate([results[cut:FIRST], results[FIRST + SLOTS[1] : WINDOW_ROWS]], axis=0)
    own = jnp.concatenate([results[:cut], results[FIRST : FIRST + SLOTS[1]]], axis=0)
    if kind == "same":
        both = finish(
            jnp.concatenate([far_rows[...], own_rows[...]], axis=0),
            jnp.concatenate([far, own], axis=0),
            gain, w_query, w_key_value, w_out,
        )
        far_result[...] = both[:ROWS]
        own_result[...] = both[ROWS:]
    else:
        far_result[...] = finish(far_rows[...], far, gain, w_query, w_key_value, w_out)
        own_result[...] = own


def tail_kernel(rows, results, gain, w_query, w_key_value, w_out, out):
    out[...] = finish(rows[...], results[...], gain, w_query, w_key_value, w_out)


def unpack_kernel(meta, table, own_same, own_cross, far_same, far_cross, block_output, input_grad):
    width = block_output.shape[1]
    token = lax.broadcasted_iota(jnp.int32, (block_output.shape[0], 4 * ROWS), 0)
    one_hot = (token == table[meta[0]]).astype(F32).astype(BF16)
    values = jnp.concatenate([own_same[...], own_cross[...], far_same[...], far_cross[...]], axis=0)
    block_output[...] = picked(one_hot, values[:, :width])
    input_grad[...] = picked(one_hot, values[:, width:])


def call(kernel, out_shapes, *operands, scratch=(), flops=0, megabytes=24):
    smem = pl.BlockSpec(memory_space=pltpu.SMEM)
    vmem = pl.BlockSpec(memory_space=pltpu.VMEM)
    outs = [jax.ShapeDtypeStruct(shape, BF16) for shape in out_shapes]
    moved = sum(x.size * x.dtype.itemsize for x in operands) + sum(x.size * 2 for x in outs)
    return pl.pallas_call(
        kernel,
        out_shape=outs,
        in_specs=[smem if x.ndim == 1 and x.dtype == jnp.int32 else vmem for x in operands],
        out_specs=[vmem] * len(outs),
        scratch_shapes=list(scratch),
        compiler_params=pltpu.CompilerParams(vmem_limit_bytes=megabytes << 20),
        cost_estimate=pl.CostEstimate(flops=flops, bytes_accessed=moved, transcendentals=0),
    )(*operands)


def on_device(inputs, out_grad, live_rows, live_cols, norm_gain, norm_bias, w_query, w_key_value, w_out):
    token_count, width = inputs.shape
    count = lax.axis_size("seq")
    position = lax.axis_index("seq")
    parity = position % 2

    frame_total = count * WT
    words = live_rows * 256 + live_cols * 16 + (jnp.arange(frame_total, dtype=jnp.int32) < HALF).astype(jnp.int32)
    around = jnp.concatenate([words[-HALF:], words, words[:HALF]])
    meta = jnp.concatenate([parity.reshape(1), lax.dynamic_slice(around, (position * WT,), (2 * WT,))])

    gain, bias = norm_gain.reshape(1, width), norm_bias.reshape(1, width)
    weights = (w_query, w_key_value, w_out)
    own_table, send_table = jnp.asarray(OWN_TOKENS[..., None]), jnp.asarray(SEND_TOKENS[..., None])
    unpack_table = jnp.asarray(np.concatenate([OWN_TOKENS, SEND_TOKENS], axis=1)[:, None, :])
    code_column, code_row = jnp.asarray(WINDOW_CODES[..., None]), jnp.asarray(WINDOW_CODES[:, None, :])

    pair = [(i, i ^ 1) for i in range(count)]
    across = [(i, (i + 1) % count if i % 2 else (i - 1) % count) for i in range(count)]

    rows_shape, heads_shape = (ROWS, 2 * width), (ROWS, 4 * width)
    product = 2 * width * width
    send_same, send_cross = call(
        pack_kernel, [rows_shape] * 2, meta, send_table, inputs, out_grad, flops=4 * ROWS * token_count * 2 * width
    )
    far_cross_rows = lax.ppermute(send_cross, "seq", across)
    far_same_rows = lax.ppermute(send_same, "seq", pair)
    own_same_rows, own_cross_rows, own_same_heads, own_cross_heads = call(
        own_kernel, [rows_shape] * 2 + [heads_shape] * 2, meta, own_table, inputs, out_grad, gain, bias, *weights,
        flops=2 * ROWS * 5 * product,
    )
    scratch = (
        pltpu.VMEM((PADDED_ROWS, 4 * width), BF16),
        pltpu.VMEM((PADDED_ROWS, 4 * width), BF16),
        pltpu.VMEM((PADDED_ROWS, GROUP_LANES), F32),
    )

    def window(kind, own_rows, own_heads, far_rows):
        return call(
            functools.partial(window_kernel, kind), [rows_shape, rows_shape if kind == "same" else heads_shape],
            meta, code_column, code_row, own_rows, own_heads, far_rows, gain, bias, *weights,
            scratch=scratch, flops=2 * ROWS * 10 * product,
        )

    far_same, own_same = window("same", own_same_rows, own_same_heads, far_same_rows)
    back_same = lax.ppermute(far_same, "seq", pair)
    far_cross, own_cross_heads = window("cross", own_cross_rows, own_cross_heads, far_cross_rows)
    back_cross = lax.ppermute(far_cross, "seq", across)
    own_cross, = call(
        tail_kernel, [rows_shape], own_cross_rows, own_cross_heads, gain, *weights, flops=ROWS * 4 * product
    )
    return tuple(
        call(
            unpack_kernel, [(token_count, width)] * 2, meta, unpack_table, own_same, own_cross, back_same, back_cross,
            flops=8 * ROWS * token_count * 2 * width,
        )
    )


def solution(mesh):
    rows = P(("group", "seq"), None)
    in_specs = (rows, rows, P("group"), P("group"), P(), P(), P(), P(), P())
    return jax.shard_map(on_device, mesh=mesh, in_specs=in_specs, out_specs=(rows, rows), check_vma=False)
```

profile of v0, /device:TPU:1, one launch (start us, length us, event | category | flops | bytes accessed | tf_op | source)
XLA Modules:
  0.0 56.0 jit_solution(5758161545674310487)
XLA Ops:
  0.6 0.7 %fusion = s32[128]{0:T(128)S(1)} fusion(s32[128]{0:T(128)} %param.17, s32[128]{0:T(128)} %param.16), kind=kLoop, calls=%fused_computation.2 | loop fusion | flops 768 | bytes 1536 | tf_op jit(solution)/shard_map/add | solution.py:285
  1.3 0.1 fusion.1
  1.4 0.1 pad_add_fusion
  1.5 0.1 dynamic_slice.3
  1.5 0.1 pad_add_fusion.1.meta
  1.6 1.1 %copy-done.5 = bf16[392,1024]{1,0:T(8,128)(2,1)S(1)} copy-done((bf16[392,1024]{1,0:T(8,128)(2,1)S(1)}, bf16[392,1024]{1,0:T(8,128)(2,1)}, u32[]{:S(2)}) %copy-start.5) | copy-done | bytes 802840
  2.8 1.1 %copy-done.7 = bf16[392,1024]{1,0:T(8,128)(2,1)S(1)} copy-done((bf16[392,1024]{1,0:T(8,128)(2,1)S(1)}, bf16[392,1024]{1,0:T(8,128)(2,1)}, u32[]{:S(2)}) %copy-start.7) | copy-done | bytes 802840
  3.9 0.9 %copy-done.9 = s32[2,224,1]{2,1,0:T(8,128)S(1)} copy-done((s32[2,224,1]{2,1,0:T(8,128)S(1)}, s32[2,224,1]{2,1,0:T(8,128)}, u32[]{:S(2)}) %copy-start.9) | copy-done | bytes 1816
  4.8 1.2 %shard_map.150 = (bf16[112,2048]{1,0:T(8,128)(2,1)S(1)}, bf16[112,2048]{1,0:T(8,128)(2,1)S(1)}) custom-call(s32[17]{0:T(128)S(1)} %pad_add_fusion.1.meta, s32[2,224,1]{2,1,0:T(8,128)S(1)} %copy-done.9, bf16[392,1024]{1,0:T(8,128)(2,1)S(1)} %copy-done.5, bf16[392,1024]{1,0:T(8,128)(2,1)S(1)} %copy-done.7), custom_call_target="tpu_custom_call" | custom-call | flops 359661568 | bytes 2524996 | tf_op jit(solution)/shard_map/pallas_call | solution.py:267
  6.1 2.7 %collective-permute-start.1 = (bf16[112,2048]{1,0:T(8,128)(2,1)S(1)}, bf16[112,2048]{1,0:T(8,128)(2,1)S(1)}, u32[]{:S(2)}, u32[]{:S(2)}) collective-permute-start(bf16[112,2048]{1,0:T(8,128)(2,1)S(1)} %get-tuple-element.18), channel_id=1, source_target_pairs={{0,15},{1,2},{2,1},{3,4},{4,3},{5,6},{6,5},{7,8},{8,7},{9,10},{10,... | collective-permute-start | bytes 1376264 | tf_op jit(solution)/shard_map/ppermute | solution.py:303
  8.7 2.9 %collective-permute-start = (bf16[112,2048]{1,0:T(8,128)(2,1)S(1)}, bf16[112,2048]{1,0:T(8,128)(2,1)S(1)}, u32[]{:S(2)}, u32[]{:S(2)}) collective-permute-start(bf16[112,2048]{1,0:T(8,128)(2,1)S(1)} %get-tuple-element.14), channel_id=1, source_target_pairs={{0,1},{1,0},{2,3},{3,2},{4,5},{5,4},{6,7},{7,6},{8,9},{9,8},{10,11... | collective-permute-start | bytes 1376264 | tf_op jit(solution)/shard_map/ppermute | solution.py:304
  11.6 2.2 %copy-done = bf16[1024,2048]{1,0:T(8,128)(2,1)S(1)} copy-done((bf16[1024,2048]{1,0:T(8,128)(2,1)S(1)}, bf16[1024,2048]{1,0:T(8,128)(2,1)}, u32[]{:S(2)}) %copy-start) | copy-done | bytes 4194328
  13.8 1.6 %copy-done.2 = bf16[1024,1024]{1,0:T(8,128)(2,1)S(1)} copy-done((bf16[1024,1024]{1,0:T(8,128)(2,1)S(1)}, bf16[1024,1024]{1,0:T(8,128)(2,1)}, u32[]{:S(2)}) %copy-start.2) | copy-done | bytes 2097176
  15.4 1.6 %copy-done.3 = bf16[1024,1024]{1,0:T(8,128)(2,1)S(1)} copy-done((bf16[1024,1024]{1,0:T(8,128)(2,1)S(1)}, bf16[1024,1024]{1,0:T(8,128)(2,1)}, u32[]{:S(2)}) %copy-start.3) | copy-done | bytes 2097176
  17.0 0.9 %copy-done.8 = s32[2,224,1]{2,1,0:T(8,128)S(1)} copy-done((s32[2,224,1]{2,1,0:T(8,128)S(1)}, s32[2,224,1]{2,1,0:T(8,128)}, u32[]{:S(2)}) %copy-start.8) | copy-done | bytes 1816
  17.9 0.7 %copy-done.10 = f32[1024]{0:T(1024)S(1)} copy-done((f32[1024]{0:T(1024)S(1)}, f32[1024]{0:T(1024)}, u32[]{:S(2)}) %copy-start.10) | copy-done | bytes 4120
  18.6 0.7 %copy-done.11 = f32[1024]{0:T(1024)S(1)} copy-done((f32[1024]{0:T(1024)S(1)}, f32[1024]{0:T(1024)}, u32[]{:S(2)}) %copy-start.11) | copy-done | bytes 4120
  19.3 3.5 %shard_map.149 = (bf16[112,2048]{1,0:T(8,128)(2,1)S(1)}, bf16[112,2048]{1,0:T(8,128)(2,1)S(1)}, bf16[112,4096]{1,0:T(8,128)(2,1)S(1)}, bf16[112,4096]{1,0:T(8,128)(2,1)S(1)}) custom-call(s32[17]{0:T(128)S(1)} %pad_add_fusion.1.meta, s32[2,224,1]{2,1,0:T(8,128)S(1)} %copy-done.8, bf16[392,1024]{1,0:T(8,128)(2,1)S(1)} %copy-done.6, ...), custom_call_target="tpu_custom_call" | custom-call | flops 2348810240 | bytes 12756804 | tf_op jit(solution)/shard_map/pallas_call | solution.py:267
  22.9 13.6 %shard_map.152 = (bf16[112,2048]{1,0:T(8,128)(2,1)S(1)}, bf16[112,4096]{1,0:T(8,128)(2,1)S(1)}) custom-call(s32[17]{0:T(128)S(1)} %pad_add_fusion.1.meta, s32[2,256,1]{2,1,0:T(8,128)S(1)} %copy-done.12, s32[2,1,256]{2,1,0:T(1,128)S(1)} %copy-done.14, bf16[112,2048]{1,0:T(8,128)(2,1)S(1)} %get-tuple-element.16.own_rows.rows, ...), custom_call_target="tpu_custom_call" | custom-call | flops 4697620480 | bytes 11612228 | tf_op jit(solution)/shard_map/pallas_call | solution.py:267
  36.4 0.1 collective-permute-start.3
  36.5 13.6 %shard_map.151 = (bf16[112,2048]{1,0:T(8,128)(2,1)S(1)}, bf16[112,2048]{1,0:T(8,128)(2,1)S(1)}) custom-call(s32[17]{0:T(128)S(1)} %pad_add_fusion.1.meta, s32[2,256,1]{2,1,0:T(8,128)S(1)} %copy-done.12, s32[2,1,256]{2,1,0:T(1,128)S(1)} %copy-done.14, bf16[112,2048]{1,0:T(8,128)(2,1)S(1)} %get-tuple-element.12.own_rows, ...), custom_call_target="tpu_custom_call" | custom-call | flops 4697620480 | bytes 11153476 | tf_op jit(solution)/shard_map/pallas_call | solution.py:267
  50.1 0.8 %collective-permute-start.2 = (bf16[112,2048]{1,0:T(8,128)(2,1)S(1)}, bf16[112,2048]{1,0:T(8,128)(2,1)S(1)}, u32[]{:S(2)}, u32[]{:S(2)}) collective-permute-start(bf16[112,2048]{1,0:T(8,128)(2,1)S(1)} %get-tuple-element.20), channel_id=1, source_target_pairs={{0,1},{1,0},{2,3},{3,2},{4,5},{5,4},{6,7},{7,6},{8,9},{9,8},{10,11... | collective-permute-start | bytes 1376264 | tf_op jit(solution)/shard_map/ppermute | solution.py:323
  50.9 2.6 %shard_map.153.own_cross = bf16[112,2048]{1,0:T(8,128)(2,1)S(1)} custom-call(bf16[112,2048]{1,0:T(8,128)(2,1)S(1)} %get-tuple-element.16.own_rows.rows, bf16[112,4096]{1,0:T(8,128)(2,1)S(1)} %get-tuple-element.19.results, f32[1,1024]{1,0:T(1,128)S(1)} %bitcast.6, bf16[1024,1024]{1,0:T(8,128)(2,1)S(1)} %copy-done.2, bf16[1024,2048]{1,0:T(8,128)(2,1)S(1)} %copy-done.1, ...), custom_call_target="tpu_custom_call" | custom-call | flops 939524096 | bytes 10227712 | tf_op jit(solution)/shard_map/pallas_call | solution.py:267
  53.6 2.4 %shard_map.154 = (bf16[392,1024]{1,0:T(8,128)(2,1)}, bf16[392,1024]{1,0:T(8,128)(2,1)}) custom-call(s32[17]{0:T(128)S(1)} %pad_add_fusion.1.meta, s32[2,1,448]{2,1,0:T(1,128)S(1)} %copy-done.13, bf16[112,2048]{1,0:T(8,128)(2,1)S(1)} %get-tuple-element.15.own_same, bf16[112,2048]{1,0:T(8,128)(2,1)S(1)} %shard_map.153.own_cross, ...), custom_call_target="tpu_custom_call" | custom-call | flops 719323136 | bytes 3444292 | tf_op jit(solution)/shard_map/pallas_call | solution.py:267
  (25 shorter events, 0.0 us)
Async XLA Ops:
  1.6 1.1 %copy-start.5 = (bf16[392,1024]{1,0:T(8,128)(2,1)S(1)}, bf16[392,1024]{1,0:T(8,128)(2,1)}, u32[]{:S(2)}) copy-start(bf16[392,1024]{1,0:T(8,128)(2,1)} %inputs.3) | copy-start | bytes 2408452
  2.8 1.1 %copy-start.7 = (bf16[392,1024]{1,0:T(8,128)(2,1)S(1)}, bf16[392,1024]{1,0:T(8,128)(2,1)}, u32[]{:S(2)}) copy-start(bf16[392,1024]{1,0:T(8,128)(2,1)} %out_grad.3) | copy-start | bytes 2408452
  3.9 0.9 %copy-start.9 = (s32[2,224,1]{2,1,0:T(8,128)S(1)}, s32[2,224,1]{2,1,0:T(8,128)}, u32[]{:S(2)}) copy-start(s32[2,224,1]{2,1,0:T(8,128)} %constant.39.clone.table) | copy-start | bytes 5380
  4.8 6.8 %copy-start.6 = (bf16[392,1024]{1,0:T(8,128)(2,1)S(1)}, bf16[392,1024]{1,0:T(8,128)(2,1)}, u32[]{:S(2)}) copy-start(bf16[392,1024]{1,0:T(8,128)(2,1)} %inputs.3) | copy-start | bytes 2408452
  6.1 16.7 %collective-permute-start.1 = (bf16[112,2048]{1,0:T(8,128)(2,1)S(1)}, bf16[112,2048]{1,0:T(8,128)(2,1)S(1)}, u32[]{:S(2)}, u32[]{:S(2)}) collective-permute-start(bf16[112,2048]{1,0:T(8,128)(2,1)S(1)} %get-tuple-element.18), channel_id=1, source_target_pairs={{0,15},{1,2},{2,1},{3,4},{4,3},{5,6},{6,5},{7,8},{8,7},{9,10},{10,... | collective-permute-start | bytes 1376264 | tf_op jit(solution)/shard_map/ppermute | solution.py:303
  8.7 27.8 %collective-permute-start = (bf16[112,2048]{1,0:T(8,128)(2,1)S(1)}, bf16[112,2048]{1,0:T(8,128)(2,1)S(1)}, u32[]{:S(2)}, u32[]{:S(2)}) collective-permute-start(bf16[112,2048]{1,0:T(8,128)(2,1)S(1)} %get-tuple-element.14), channel_id=1, source_target_pairs={{0,1},{1,0},{2,3},{3,2},{4,5},{5,4},{6,7},{7,6},{8,9},{9,8},{10,11... | collective-permute-start | bytes 1376264 | tf_op jit(solution)/shard_map/ppermute | solution.py:304
  11.6 2.2 %copy-start = (bf16[1024,2048]{1,0:T(8,128)(2,1)S(1)}, bf16[1024,2048]{1,0:T(8,128)(2,1)}, u32[]{:S(2)}) copy-start(bf16[1024,2048]{1,0:T(8,128)(2,1)} %w_key_value.7) | copy-start | bytes 12582916
  13.8 1.6 %copy-start.2 = (bf16[1024,1024]{1,0:T(8,128)(2,1)S(1)}, bf16[1024,1024]{1,0:T(8,128)(2,1)}, u32[]{:S(2)}) copy-start(bf16[1024,1024]{1,0:T(8,128)(2,1)} %w_query.7) | copy-start | bytes 6291460
  15.4 1.6 %copy-start.3 = (bf16[1024,1024]{1,0:T(8,128)(2,1)S(1)}, bf16[1024,1024]{1,0:T(8,128)(2,1)}, u32[]{:S(2)}) copy-start(bf16[1024,1024]{1,0:T(8,128)(2,1)} %w_out.7) | copy-start | bytes 6291460
  17.0 0.9 %copy-start.8 = (s32[2,224,1]{2,1,0:T(8,128)S(1)}, s32[2,224,1]{2,1,0:T(8,128)}, u32[]{:S(2)}) copy-start(s32[2,224,1]{2,1,0:T(8,128)} %constant.38.clone.table) | copy-start | bytes 5380
  17.9 0.7 %copy-start.10 = (f32[1024]{0:T(1024)S(1)}, f32[1024]{0:T(1024)}, u32[]{:S(2)}) copy-start(f32[1024]{0:T(1024)} %param.18) | copy-start | bytes 12292
  18.6 0.7 %copy-start.11 = (f32[1024]{0:T(1024)S(1)}, f32[1024]{0:T(1024)}, u32[]{:S(2)}) copy-start(f32[1024]{0:T(1024)} %param.19) | copy-start | bytes 12292
  19.3 3.5 %copy-start.1 = (bf16[1024,2048]{1,0:T(8,128)(2,1)S(1)}, bf16[1024,2048]{1,0:T(8,128)(2,1)}, u32[]{:S(2)}) copy-start(bf16[1024,2048]{1,0:T(8,128)(2,1)} %w_key_value.7) | copy-start | bytes 12582916
  19.3 3.5 %copy-start.4 = (bf16[1024,1024]{1,0:T(8,128)(2,1)S(1)}, bf16[1024,1024]{1,0:T(8,128)(2,1)}, u32[]{:S(2)}) copy-start(bf16[1024,1024]{1,0:T(8,128)(2,1)} %w_out.7) | copy-start | bytes 6291460
  19.3 3.5 %copy-start.12 = (s32[2,256,1]{2,1,0:T(8,128)S(1)}, s32[2,256,1]{2,1,0:T(8,128)}, u32[]{:S(2)}) copy-start(s32[2,256,1]{2,1,0:T(8,128)} %constant.41.clone.code_column) | copy-start | bytes 6148
  19.3 3.6 %copy-start.14 = (s32[2,1,256]{2,1,0:T(1,128)S(1)}, s32[2,1,256]{2,1,0:T(1,128)}, u32[]{:S(2)}) copy-start(s32[2,1,256]{2,1,0:T(1,128)} %constant.42.clone.code_row) | copy-start | bytes 6148
  36.4 17.1 %collective-permute-start.3 = (bf16[112,2048]{1,0:T(8,128)(2,1)S(1)}, bf16[112,2048]{1,0:T(8,128)(2,1)S(1)}, u32[]{:S(2)}, u32[]{:S(2)}) collective-permute-start(bf16[112,2048]{1,0:T(8,128)(2,1)S(1)} %get-tuple-element.21), channel_id=1, source_target_pairs={{0,15},{1,2},{2,1},{3,4},{4,3},{5,6},{6,5},{7,8},{8,7},{9,10},{10,... | collective-permute-start | bytes 1376264 | tf_op jit(solution)/shard_map/ppermute | solution.py:325
  50.1 3.4 %collective-permute-start.2 = (bf16[112,2048]{1,0:T(8,128)(2,1)S(1)}, bf16[112,2048]{1,0:T(8,128)(2,1)S(1)}, u32[]{:S(2)}, u32[]{:S(2)}) collective-permute-start(bf16[112,2048]{1,0:T(8,128)(2,1)S(1)} %get-tuple-element.20), channel_id=1, source_target_pairs={{0,1},{1,0},{2,3},{3,2},{4,5},{5,4},{6,7},{7,6},{8,9},{9,8},{10,11... | collective-permute-start | bytes 1376264 | tf_op jit(solution)/shard_map/ppermute | solution.py:323
  50.9 2.6 %copy-start.13 = (s32[2,1,448]{2,1,0:T(1,128)S(1)}, s32[2,1,448]{2,1,0:T(1,128)}, u32[]{:S(2)}) copy-start(s32[2,1,448]{2,1,0:T(1,128)} %constant.40.clone.table) | copy-start | bytes 10756
where the time goes:
time: 56.5 us; the launch traced here: 56 us
  Pallas kernels  36.9 us (65%)
  local copies, waits for them, and re-layouts  11.1 us (20%)
  starting transfers between devices  6.4 us (11%)
  other arithmetic  0.83 us (1%)
  between operations  0.78 us (1%)
    pallas_call x6, Pallas kernels, call(): pl.pallas_call(kernel, out_shape=outs, in_specs=[smem if x.ndim == 1 and...  36.9 us
    unnamed x30, local copies, waits for them, and re-layouts  10.9 us
    ppermute x1, starting transfers between devices, on_device(): far_same_rows = lax.ppermute(send_same, 'seq', pair)  2.85 us
    ppermute x1, starting transfers between devices, on_device(): far_cross_rows = lax.ppermute(send_cross, 'seq', across)  2.68 us
  transfers between devices with their start and end apart: 4, of which 0 were waited for; matrix products, arithmetic and copies ran while one was open for 0% of the time, Pallas kernels for 59%

commit v1 on v0

v1 whole, which is shorter than its diff:
```python
import functools

import jax
import jax.numpy as jnp
import numpy as np
from jax import lax
from jax.experimental import pallas as pl
from jax.experimental.pallas import tpu as pltpu
from jax.sharding import PartitionSpec as P

HEAD_DIM = 32
WT = 8
WH = 7
WW = 7
CELLS = WH * WW
HALF = WT // 2
EPSILON = 1e-05
GROUP_LANES = 128
HEADS_PER_GROUP = GROUP_LANES // HEAD_DIM
SLOTS = (64, 48)
ROWS = sum(SLOTS)
FIRST = 2 * SLOTS[0]
SECOND = 2 * SLOTS[1]
WINDOW_ROWS = FIRST + SECOND
PADDED_ROWS = 2 * GROUP_LANES
MASKED = -1e30
SCALE = HEAD_DIM ** (-0.5)
LOG2E = float(np.log2(np.e))
BF16 = jnp.bfloat16
F32 = jnp.float32
NT = (((1,), (1,)), ((), ()))


def quadrant_cells(quadrant):
    rows = range(WH // 2) if quadrant & 2 else range(WH // 2, WH)
    cols = range(WW // 2) if quadrant & 1 else range(WW // 2, WW)
    return [(row, col) for row in rows for col in cols]


def half_slots(units):
    slots = []
    for quadrant, room in zip(units, SLOTS):
        entries = [(frame, row, col) for frame in range(HALF) for row, col in quadrant_cells(quadrant)]
        slots += entries + [None] * (room - len(entries))
    return slots


def tables():
    takes = {"last": (0, 3), "first": (1, 2)}
    gives = {"last": (1, 2), "first": (0, 3)}

    def tokens(side, units):
        shift = HALF if side == "last" else 0
        return [-1 if s is None else (s[0] + shift) * CELLS + s[1] * WW + s[2] for s in half_slots(units)]

    def codes(slots, second_half):
        return [-1 if s is None else (s[0] + HALF * second_half) * 64 + s[1] * 8 + s[2] for s in slots]

    own, send, window = [], [], []
    for parity in range(2):
        sides = ("last", "first") if parity == 0 else ("first", "last")
        own.append(sum((tokens(side, takes[side]) for side in sides), []))
        send.append(sum((tokens(side, gives[side]) for side in sides), []))
    for side in ("first", "last"):
        slots = half_slots(takes[side])
        mine = codes(slots, side == "first")
        theirs = codes(slots, side == "last")
        cut = SLOTS[0]
        rows = mine[:cut] + theirs[:cut] + mine[cut:] + theirs[cut:]
        window.append(rows + [-1] * (PADDED_ROWS - len(rows)))
    return np.array(own, np.int32), np.array(send, np.int32), np.array(window, np.int32)


OWN_TOKENS, SEND_TOKENS, WINDOW_CODES = tables()


def normalized(values_in):
    values = values_in.astype(F32)
    centred = values - jnp.mean(values, axis=-1, keepdims=True)
    inv_dev = lax.rsqrt(jnp.mean(centred * centred, axis=-1, keepdims=True) + EPSILON)
    return centred * inv_dev, inv_dev


def one_hot_rows(token_column, token_count):
    lanes = lax.broadcasted_iota(jnp.int32, (token_column.shape[0], token_count), 1)
    return (lanes == token_column).astype(F32).astype(BF16)


def picked(one_hot, values):
    return jnp.dot(one_hot, values, preferred_element_type=F32).astype(BF16)


def side_of(kind, position):
    parity = lax.rem(position, 2)
    return 1 - parity if kind == "same" else parity


def pack_kernel(position, table, inputs, out_grad, same, cross, values, grads, sems):
    width = inputs.shape[1]
    copies = [
        pltpu.make_async_copy(source, target, sems.at[place])
        for place, (source, target) in enumerate(((inputs, values), (out_grad, grads)))
    ]
    for copy in copies:
        copy.start()
    one_hot = one_hot_rows(table[lax.rem(position[0], 2)], inputs.shape[0])
    for place, source in enumerate((values, grads)):
        copies[place].wait()
        rows = picked(one_hot, source[...])
        columns = slice(place * width, (place + 1) * width)
        same[:, columns] = rows[:ROWS]
        cross[:, columns] = rows[ROWS:]


def hidden_of(values, gain, bias):
    unit, _ = normalized(values)
    return (unit * gain[...] + bias[...]).astype(BF16)


def own_kernel(
    position, table, inputs, out_grad, gain, bias, w_query, w_key_value, w_out,
    rows_same, rows_cross, heads_same, heads_cross, query_copy, pair_copy, out_copy, sems,
):
    width = inputs.shape[1]
    halves = [pl.ds(part * width, width) for part in range(2)]
    copies = [pltpu.make_async_copy(w_query, query_copy, sems.at[0])]
    copies += [
        pltpu.make_async_copy(w_key_value.at[:, part], pair_copy.at[:, part], sems.at[1 + index])
        for index, part in enumerate(halves)
    ]
    copies += [pltpu.make_async_copy(w_out, out_copy, sems.at[3])]
    for copy in copies:
        copy.start()
    one_hot = one_hot_rows(table[lax.rem(position[0], 2)], inputs.shape[0])
    values = picked(one_hot, inputs[...])
    hidden = hidden_of(values, gain, bias)
    grads = picked(one_hot, out_grad[...])
    for place, rows in enumerate((values, grads)):
        columns = slice(place * width, (place + 1) * width)
        rows_same[:, columns] = rows[:ROWS]
        rows_cross[:, columns] = rows[ROWS:]
    for part in range(3):
        copies[part].wait()
        weights = query_copy[...] if part == 0 else pair_copy[:, halves[part - 1]]
        result = jnp.dot(hidden, weights, preferred_element_type=F32).astype(BF16)
        columns = slice(part * width, (part + 1) * width)
        heads_same[:, columns] = result[:ROWS]
        heads_cross[:, columns] = result[ROWS:]
    copies[3].wait()


def cell_codes(slots, place, frames):
    frame = slots >> 6
    word = jnp.zeros_like(slots)
    for index, frame_word in enumerate(frames):
        word = jnp.where(frame == index, frame_word, word)
    row, col = (slots >> 3) & 7, slots & 7
    live = (slots >= 0) & (row < (word >> 8)) & (col < ((word >> 4) & 15))
    return jnp.where(live, word & 1, -1 - place)


def head_rows(h):
    return slice(h * HEAD_DIM, (h + 1) * HEAD_DIM)


def head_lanes(h):
    return slice(h * GROUP_LANES, (h + 1) * GROUP_LANES)


def block_diagonal(values):
    zero = jnp.zeros((HEAD_DIM, GROUP_LANES), values.dtype)
    return jnp.concatenate(
        [
            jnp.concatenate([values[head_rows(r)] if r == h else zero for r in range(HEADS_PER_GROUP)], axis=0)
            for h in range(HEADS_PER_GROUP)
        ],
        axis=1,
    )


def score_stage(unit, group, groups, count, heads, grads_t, query_t, scores, grad_probs):
    base = unit * GROUP_LANES
    keys = slice(base, base + count)
    query = heads[group, base : base + GROUP_LANES].T
    query_t[...] = query
    grad = grads_t[unit, pl.ds(pl.multiple_of(group * GROUP_LANES, GROUP_LANES), GROUP_LANES)]
    score = jnp.dot(heads[groups + group, keys], block_diagonal(query), preferred_element_type=F32)
    grad_prob = jnp.dot(heads[2 * groups + group, keys], block_diagonal(grad), preferred_element_type=F32)
    for h in range(HEADS_PER_GROUP):
        scores[h] = score[:, head_lanes(h)]
        grad_probs[h] = grad_prob[:, head_lanes(h)]


def softmax_stage(unit, count, bias_of, scores, grad_probs, probs, grad_scores):
    for h in range(HEADS_PER_GROUP):
        score = scores[h] * (SCALE * LOG2E) + bias_of[unit, :count]
        raw = jnp.exp2(score - jnp.max(score, axis=0, keepdims=True))
        inverse = 1.0 / jnp.sum(raw, axis=0, keepdims=True)
        grad_prob = grad_probs[h]
        row_dot = jnp.sum(raw * grad_prob, axis=0, keepdims=True) * inverse
        probs[h] = (raw * inverse).astype(BF16)
        grad_scores[h] = (raw * ((grad_prob - row_dot) * (inverse * SCALE))).astype(BF16)


def product_stage(unit, group, groups, count, heads, grads_t, query_t, probs, grad_scores, results):
    base = unit * GROUP_LANES
    keys = slice(base, base + count)
    grad = grads_t[unit, pl.ds(pl.multiple_of(group * GROUP_LANES, GROUP_LANES), GROUP_LANES)]
    key_t, value_t = heads[groups + group, keys].T, heads[2 * groups + group, keys].T

    def per_key(left, right):
        left = jnp.concatenate([left[h] for h in range(HEADS_PER_GROUP)], axis=1)
        return lax.dot_general(left, block_diagonal(right), NT, preferred_element_type=F32).astype(BF16)

    def per_query(left, right):
        parts = [jnp.dot(left[head_rows(h)], right[h], preferred_element_type=F32) for h in range(HEADS_PER_GROUP)]
        return jnp.concatenate(parts, axis=0).T[:count].astype(BF16)

    results[group, keys] = per_query(value_t, probs)
    results[groups + group, keys] = per_query(key_t, grad_scores)
    results[2 * groups + group, keys] = per_key(grad_scores, query_t[...])
    results[3 * groups + group, keys] = per_key(probs, grad)


def finish(values, grads, results, gain, w_query, w_key_value, w_out):
    width = values.shape[1]
    rows = values.shape[0]
    block_output = values.astype(F32) + jnp.dot(results[:, :width], w_out[...], preferred_element_type=F32)
    fill = -rows % GROUP_LANES
    moves = jnp.concatenate([results[:, width:], jnp.zeros((fill, 3 * width), BF16)], axis=0)
    grad_hidden = lax.dot_general(w_query[...], moves[:, :width], NT, preferred_element_type=F32)
    grad_hidden = grad_hidden + lax.dot_general(w_key_value[...], moves[:, width:], NT, preferred_element_type=F32)
    grad_hidden = grad_hidden.T[:rows]
    unit, inv_dev = normalized(values)
    scaled = grad_hidden * gain[...]
    centred = scaled - jnp.mean(scaled, axis=-1, keepdims=True)
    norm_grad = inv_dev * (centred - unit * jnp.mean(scaled * unit, axis=-1, keepdims=True))
    return block_output.astype(BF16), (grads.astype(F32) + norm_grad).astype(BF16)


def window_kernel(
    kind, position, live_rows, live_cols, code_column, code_row, own_rows, own_heads, far_rows, other_far,
    gain, bias, w_query, w_key_value, w_out, far_result, own_moves, other_heads,
    heads, window_grads, grads_t, results, bias_of, query_t0, query_t1, *stages,
):
    width = far_rows.shape[1] // 2
    groups = width // GROUP_LANES
    cut, second = SLOTS[0], FIRST + SLOTS[1]
    side = side_of(kind, position[0])
    total = live_rows.shape[0]
    frames = []
    for index in range(WT):
        frame = lax.rem(position[0] * WT + (side * 2 - 1) * HALF + index + total, total)
        frames.append(live_rows[frame] * 256 + live_cols[frame] * 16 + (frame < HALF).astype(jnp.int32))
    by_key = cell_codes(code_column[side], lax.broadcasted_iota(jnp.int32, (PADDED_ROWS, 1), 0), frames)
    by_query = cell_codes(code_row[side], lax.broadcasted_iota(jnp.int32, (1, PADDED_ROWS), 1), frames)
    for unit in range(2):
        block = slice(unit * GROUP_LANES, (unit + 1) * GROUP_LANES)
        bias_of[unit] = jnp.where(by_key[block] == by_query[:, block], 0.0, MASKED)

    window_grads[:cut] = own_rows[:cut, width:]
    window_grads[cut:FIRST] = far_rows[:cut, width:]
    window_grads[FIRST:second] = own_rows[cut:, width:]
    window_grads[second:WINDOW_ROWS] = far_rows[cut:, width:]
    window_grads[WINDOW_ROWS:] = jnp.zeros((PADDED_ROWS - WINDOW_ROWS, width), BF16)
    turned = lax.dot_general(w_out[...], window_grads[...], NT, preferred_element_type=F32).astype(BF16)
    for unit in range(2):
        grads_t[unit] = turned[:, unit * GROUP_LANES : (unit + 1) * GROUP_LANES]

    def place(block, own, far):
        heads[block, :cut] = own[:cut]
        heads[block, cut:FIRST] = far[:cut]
        heads[block, FIRST:second] = own[cut:]
        heads[block, second:WINDOW_ROWS] = far[cut:]

    for block in range(groups):
        heads[block, WINDOW_ROWS:] = jnp.zeros((PADDED_ROWS - WINDOW_ROWS, GROUP_LANES), BF16)
    if kind == "cross":
        hidden = hidden_of(jnp.concatenate([far_rows[:, :width], other_far[:, :width]], axis=0), gain, bias)
    for part in range(3):
        columns = slice(part * width, (part + 1) * width)
        if kind == "cross":
            weights = w_query[...] if part == 0 else w_key_value[:, slice((part - 1) * width, part * width)]
            result = jnp.dot(hidden, weights, preferred_element_type=F32).astype(BF16)
            far = result[:ROWS]
            other_heads[:, columns] = result[ROWS:]
        else:
            far = other_far[:, columns]
        for group in range(groups):
            lanes = slice(group * GROUP_LANES, (group + 1) * GROUP_LANES)
            first = part * width + group * GROUP_LANES
            place(part * groups + group, own_heads[:, first : first + GROUP_LANES], far[:, lanes])

    query_t = (query_t0, query_t1)
    counts = (FIRST, SECOND)
    scores, grad_probs, probs, grad_scores = stages[0:2], stages[2:4], stages[4:6], stages[6:8]

    def score(unit, group):
        score_stage(unit, group, groups, counts[unit], heads, grads_t, query_t[unit], scores[unit], grad_probs[unit])

    def softmax(unit):
        softmax_stage(unit, counts[unit], bias_of, scores[unit], grad_probs[unit], probs[unit], grad_scores[unit])

    def product(unit, group):
        product_stage(
            unit, group, groups, counts[unit], heads, grads_t, query_t[unit], probs[unit], grad_scores[unit], results
        )

    probs[1][...] = jnp.zeros_like(probs[1])
    grad_scores[1][...] = jnp.zeros_like(grad_scores[1])
    query_t[1][...] = jnp.zeros_like(query_t[1])
    score(0, 0)

    def body(group, carry):
        product(1, jnp.maximum(group - 1, 0))
        score(1, group)
        softmax(0)
        product(0, group)
        score(0, jnp.minimum(group + 1, groups - 1))
        softmax(1)
        return carry

    lax.fori_loop(0, groups, body, 0)
    product(1, groups - 1)

    def rows_of(first, last):
        return jnp.concatenate(
            [
                jnp.concatenate([results[block, first[0] : first[1]], results[block, last[0] : last[1]]], axis=0)
                for block in range(4 * groups)
            ],
            axis=1,
        )

    own_moves[...] = rows_of((0, cut), (FIRST, second))
    block_output, input_grad = finish(
        far_rows[:, :width], far_rows[:, width:], rows_of((cut, FIRST), (second, WINDOW_ROWS)),
        gain, w_query, w_key_value, w_out,
    )
    far_result[:, :width] = block_output
    far_result[:, width:] = input_grad


def tail_kernel(rows_same, rows_cross, moves_same, moves_cross, gain, w_query, w_key_value, w_out, out):
    width = rows_same.shape[1] // 2
    rows = jnp.concatenate([rows_same[...], rows_cross[...]], axis=0)
    moves = jnp.concatenate([moves_same[...], moves_cross[...]], axis=0)
    block_output, input_grad = finish(rows[:, :width], rows[:, width:], moves, gain, w_query, w_key_value, w_out)
    out[:, :width] = block_output
    out[:, width:] = input_grad


def unpack_kernel(position, table, own, far_same, far_cross, block_output, input_grad, outputs, sems):
    width = block_output.shape[1]
    chunk = width // 2
    token = lax.broadcasted_iota(jnp.int32, (block_output.shape[0], 4 * ROWS), 0)
    one_hot = (token == table[lax.rem(position[0], 2)]).astype(F32).astype(BF16)
    copies = []
    for index in range(4):
        columns = slice(index * chunk, (index + 1) * chunk)
        values = jnp.concatenate([own[:, columns], far_same[:, columns], far_cross[:, columns]], axis=0)
        outputs[index] = picked(one_hot, values)
        target = block_output if index < 2 else input_grad
        copies.append(
            pltpu.make_async_copy(outputs.at[index], target.at[:, pl.ds(index % 2 * chunk, chunk)], sems.at[index])
        )
        copies[-1].start()
    for copy in copies:
        copy.wait()


SMEM, VMEM, HBM = pltpu.SMEM, pltpu.VMEM, pltpu.HBM


def call(kernel, outs, *operands, scratch=(), flops=0, megabytes=24):
    spaces, operands = zip(*operands)
    out_spaces, shapes = zip(*outs)
    outs = [jax.ShapeDtypeStruct(shape, BF16) for shape in shapes]
    moved = sum(x.size * x.dtype.itemsize for x in operands) + sum(x.size * 2 for x in outs)
    return pl.pallas_call(
        kernel,
        out_shape=outs,
        in_specs=[pl.BlockSpec(memory_space=space) for space in spaces],
        out_specs=[pl.BlockSpec(memory_space=space) for space in out_spaces],
        scratch_shapes=list(scratch),
        compiler_params=pltpu.CompilerParams(vmem_limit_bytes=megabytes << 20),
        cost_estimate=pl.CostEstimate(flops=flops, bytes_accessed=moved, transcendentals=0),
    )(*operands)


def on_device(inputs, out_grad, live_rows, live_cols, norm_gain, norm_bias, w_query, w_key_value, w_out):
    token_count, width = inputs.shape
    groups = width // GROUP_LANES
    count = lax.axis_size("seq")
    position = (SMEM, lax.axis_index("seq").reshape(1))
    live = ((SMEM, live_rows), (SMEM, live_cols))
    norm = ((VMEM, norm_gain.reshape(1, width)), (VMEM, norm_bias.reshape(1, width)))
    own_table, send_table = (VMEM, jnp.asarray(OWN_TOKENS[..., None])), (VMEM, jnp.asarray(SEND_TOKENS[..., None]))
    unpack_table = (VMEM, jnp.asarray(np.concatenate([OWN_TOKENS, SEND_TOKENS], axis=1)[:, None, :]))
    codes = (VMEM, jnp.asarray(WINDOW_CODES[..., None])), (VMEM, jnp.asarray(WINDOW_CODES[:, None, :]))

    pair = [(i, i ^ 1) for i in range(count)]
    across = [(i, (i + 1) % count if i % 2 else (i - 1) % count) for i in range(count)]

    rows_out, heads_out, moves_out = (VMEM, (ROWS, 2 * width)), (VMEM, (ROWS, 3 * width)), (VMEM, (ROWS, 4 * width))
    product = 2 * width * width
    send_same, send_cross, values, grads = call(
        pack_kernel,
        [rows_out] * 2 + [(VMEM, inputs.shape)] * 2,
        position, send_table, (HBM, inputs), (HBM, out_grad),
        scratch=[pltpu.SemaphoreType.DMA((2,))],
        flops=4 * ROWS * token_count * 2 * width,
    )
    far_cross_rows = lax.ppermute(send_cross, "seq", across)
    far_same_rows = lax.ppermute(send_same, "seq", pair)
    own_same_rows, own_cross_rows, own_same_heads, own_cross_heads, *weights = call(
        own_kernel,
        [rows_out] * 2 + [heads_out] * 2 + [(VMEM, w.shape) for w in (w_query, w_key_value, w_out)],
        position, own_table, (VMEM, values), (VMEM, grads), *norm, (HBM, w_query), (HBM, w_key_value), (HBM, w_out),
        scratch=[pltpu.SemaphoreType.DMA((4,))],
        flops=2 * ROWS * 4 * product,
    )
    weights = [(VMEM, w) for w in weights]

    stages = [VMEM((HEADS_PER_GROUP, n, GROUP_LANES), kind) for kind in (F32, F32, BF16, BF16) for n in (FIRST, SECOND)]
    scratch = [
        VMEM((3 * groups, PADDED_ROWS, GROUP_LANES), BF16),
        VMEM((PADDED_ROWS, width), BF16),
        VMEM((2, width, GROUP_LANES), BF16),
        VMEM((4 * groups, PADDED_ROWS, GROUP_LANES), BF16),
        VMEM((2, GROUP_LANES, GROUP_LANES), F32),
        VMEM((GROUP_LANES, GROUP_LANES), BF16),
        VMEM((GROUP_LANES, GROUP_LANES), BF16),
        *stages,
    ]

    def window(kind, own_rows, own_heads, far_rows, other_far):
        outs = [rows_out, moves_out, heads_out if kind == "cross" else (VMEM, (16, GROUP_LANES))]
        arrays = [(VMEM, x) for x in (own_rows, own_heads, far_rows, other_far)]
        return call(
            functools.partial(window_kernel, kind), outs, position, *live, *codes, *arrays, *norm, *weights,
            scratch=scratch, flops=2 * ROWS * 10 * product,
        )

    far_cross, own_cross_moves, far_same_heads = window(
        "cross", own_cross_rows, own_cross_heads, far_cross_rows, far_same_rows
    )
    back_cross = lax.ppermute(far_cross, "seq", across)
    far_same, own_same_moves, _ = window("same", own_same_rows, own_same_heads, far_same_rows, far_same_heads)
    back_same = lax.ppermute(far_same, "seq", pair)
    arrays = [(VMEM, x) for x in (own_same_rows, own_cross_rows, own_same_moves, own_cross_moves)]
    (own,) = call(
        tail_kernel, [(VMEM, (2 * ROWS, 2 * width))], *arrays, norm[0], *weights, flops=2 * ROWS * 4 * product
    )
    arrays = [(VMEM, x) for x in (own, back_same, back_cross)]
    return tuple(
        call(
            unpack_kernel, [(HBM, (token_count, width))] * 2, position, unpack_table, *arrays,
            scratch=[VMEM((4, token_count, width // 2), BF16), pltpu.SemaphoreType.DMA((4,))],
            flops=8 * ROWS * token_count * 2 * width,
        )
    )


def solution(mesh):
    rows = P(("group", "seq"), None)
    in_specs = (rows, rows, P("group"), P("group"), P(), P(), P(), P(), P())
    return jax.shard_map(on_device, mesh=mesh, in_specs=in_specs, out_specs=(rows, rows), check_vma=False)
```

time: 56.5 us -> 57.9 us (1.025)
  waiting for transfers between devices: 0.01 us -> 10 us
  Pallas kernels: 36.9 us -> 29.3 us
  other arithmetic: 0.83 us -> 0 us
    ppermute x1, waiting for transfers between devices: 0.01 us -> 10 us  [on_device(): back_cross = lax.ppermute(far_cross, 'seq', across)]
    pallas_call x6, Pallas kernels: 36.9 us -> 29.3 us  [call(): pl.pallas_call(kernel, out_shape=outs, in_specs=[pl.BlockSpec(memory_spac...]
    ppermute x1, starting transfers between devices: 2.85 us -> 0.08 us  [on_device(): far_same_rows = lax.ppermute(send_same, 'seq', pair)]
    ppermute x1, starting transfers between devices: 0.81 us -> 3.53 us  [on_device(): back_same = lax.ppermute(far_same, 'seq', pair)]
    add x1 -> x0, other arithmetic: 0.68 us -> none  [on_device(): live_rows * 256 + live_cols * 16]
    unnamed x30 -> x28, local copies, waits for them, and re-layouts: 10.9 us -> 10.9 us
  transfers between devices with their start and end apart: 4 -> 4, of which waited for: 0 -> 1; matrix products, arithmetic and copies ran while one was open for 0% -> 0% of each run, Pallas kernels for 59% -> 12%
where the time goes in v1:
time: 57.9 us; the launch traced here: 57.5 us
  Pallas kernels  29.3 us (51%)
  local copies, waits for them, and re-layouts  10.9 us (19%)
  waiting for transfers between devices  10 us (17%)
  starting transfers between devices  6.27 us (11%)
  between operations  0.91 us (2%)
    pallas_call x6, Pallas kernels, call(): pl.pallas_call(kernel, out_shape=outs, in_specs=[pl.BlockSpec(memory_spac...  29.3 us
    unnamed x28, local copies, waits for them, and re-layouts  10.9 us
    ppermute x1, waiting for transfers between devices, on_device(): back_cross = lax.ppermute(far_cross, 'seq', across)  10 us
    ppermute x1, starting transfers between devices, on_device(): back_same = lax.ppermute(far_same, 'seq', pair)  3.53 us
    ppermute x1, starting transfers between devices, on_device(): far_cross_rows = lax.ppermute(send_cross, 'seq', across)  2.66 us
  transfers between devices with their start and end apart: 4, of which 1 were waited for; matrix products, arithmetic and copies ran while one was open for 0% of the time, Pallas kernels for 12%

profile of v1, /device:TPU:1, one launch (start us, length us, event | category | flops | bytes accessed | tf_op | source)
XLA Modules:
  0.0 57.5 jit_solution(220129129172237793)
XLA Ops:
  0.6 0.0 copy-start.3
  0.6 1.1 %copy-done.3 = bf16[392,1024]{1,0:T(8,128)(2,1)S(1)} copy-done((bf16[392,1024]{1,0:T(8,128)(2,1)S(1)}, bf16[392,1024]{1,0:T(8,128)(2,1)}, u32[]{:S(2)}) %copy-start.3) | copy-done | bytes 802840
  1.8 1.1 %copy-done.4 = bf16[392,1024]{1,0:T(8,128)(2,1)S(1)} copy-done((bf16[392,1024]{1,0:T(8,128)(2,1)S(1)}, bf16[392,1024]{1,0:T(8,128)(2,1)}, u32[]{:S(2)}) %copy-start.4) | copy-done | bytes 802840
  2.9 0.9 %copy-done.6 = s32[2,224,1]{2,1,0:T(8,128)S(1)} copy-done((s32[2,224,1]{2,1,0:T(8,128)S(1)}, s32[2,224,1]{2,1,0:T(8,128)}, u32[]{:S(2)}) %copy-start.6) | copy-done | bytes 1816
  3.9 1.1 %shard_map.149 = (bf16[112,2048]{1,0:T(8,128)(2,1)S(1)}, bf16[112,2048]{1,0:T(8,128)(2,1)S(1)}, bf16[392,1024]{1,0:T(8,128)(2,1)S(1)}, bf16[392,1024]{1,0:T(8,128)(2,1)S(1)}) custom-call(s32[1]{0:T(128)} %bitcast.position, s32[2,224,1]{2,1,0:T(8,128)S(1)} %copy-done.6, bf16[392,1024]{1,0:T(8,128)(2,1)S(1)} %copy-done.3, bf16[392,1024]{1,0:T(8,128)(2,1)S(1)} %copy-done.4), custom_call_target="tpu_custom_call" | custom-call | flops 359661568 | bytes 4130564 | tf_op jit(solution)/shard_map/pallas_call | solution.py:380
  4.9 0.1 collective-permute-start
  5.0 2.7 %collective-permute-start.1 = (bf16[112,2048]{1,0:T(8,128)(2,1)S(1)}, bf16[112,2048]{1,0:T(8,128)(2,1)S(1)}, u32[]{:S(2)}, u32[]{:S(2)}) collective-permute-start(bf16[112,2048]{1,0:T(8,128)(2,1)S(1)} %get-tuple-element.25), channel_id=1, source_target_pairs={{0,15},{1,2},{2,1},{3,4},{4,3},{5,6},{6,5},{7,8},{8,7},{9,10},{10,... | collective-permute-start | bytes 1376264 | tf_op jit(solution)/shard_map/ppermute | solution.py:414
  7.7 2.2 %copy-done = bf16[1024,2048]{1,0:T(8,128)(2,1)S(1)} copy-done((bf16[1024,2048]{1,0:T(8,128)(2,1)S(1)}, bf16[1024,2048]{1,0:T(8,128)(2,1)}, u32[]{:S(2)}) %copy-start) | copy-done | bytes 4194328
  9.9 1.6 %copy-done.1 = bf16[1024,1024]{1,0:T(8,128)(2,1)S(1)} copy-done((bf16[1024,1024]{1,0:T(8,128)(2,1)S(1)}, bf16[1024,1024]{1,0:T(8,128)(2,1)}, u32[]{:S(2)}) %copy-start.1) | copy-done | bytes 2097176
  11.5 1.6 %copy-done.2 = bf16[1024,1024]{1,0:T(8,128)(2,1)S(1)} copy-done((bf16[1024,1024]{1,0:T(8,128)(2,1)S(1)}, bf16[1024,1024]{1,0:T(8,128)(2,1)}, u32[]{:S(2)}) %copy-start.2) | copy-done | bytes 2097176
  13.1 0.9 %copy-done.5 = s32[2,224,1]{2,1,0:T(8,128)S(1)} copy-done((s32[2,224,1]{2,1,0:T(8,128)S(1)}, s32[2,224,1]{2,1,0:T(8,128)}, u32[]{:S(2)}) %copy-start.5) | copy-done | bytes 1816
  14.0 0.7 %copy-done.7 = f32[1024]{0:T(1024)S(1)} copy-done((f32[1024]{0:T(1024)S(1)}, f32[1024]{0:T(1024)}, u32[]{:S(2)}) %copy-start.7) | copy-done | bytes 4120
  14.7 0.7 %copy-done.8 = f32[1024]{0:T(1024)S(1)} copy-done((f32[1024]{0:T(1024)S(1)}, f32[1024]{0:T(1024)}, u32[]{:S(2)}) %copy-start.8) | copy-done | bytes 4120
  15.4 4.1 %shard_map.150 = (bf16[112,2048]{1,0:T(8,128)(2,1)S(1)}, bf16[112,2048]{1,0:T(8,128)(2,1)S(1)}, bf16[112,3072]{1,0:T(8,128)(2,1)S(1)}, bf16[112,3072]{1,0:T(8,12...) custom-call(s32[1]{0:T(128)} %bitcast.position, ...), custom_call_target="tpu_custom_call" | custom-call | flops 1879048192 | bytes 20686596 | tf_op jit(solution)/shard_map/pallas_call | solution.py:380
  19.5 0.0 collective-permute-done.other_far.far_rows
  19.5 0.0 collective-permute-done.1.far_rows
  19.5 10.5 %shard_map.151 = (bf16[112,2048]{1,0:T(8,128)(2,1)S(1)}, bf16[112,4096]{1,0:T(8,128)(2,1)S(1)}, bf16[112,3072]{1,0:T(8,128)(2,1)S(1)}) custom-call(s32[1]{0:T(128)} %bitcast.position, s32[128]{0:T(128)S(1)} %copy-done.9, s32[128]{0:T(128)S(1)} %copy-done.10, s32[2,256,1]{2,1,0:T(8,128)S(1)} %copy-done.11, s32[2,1,256]{2,1,0:T(1,128)S(1)} %copy-done.13, ...), custom_call_target="tpu_custom_call" | custom-call | flops 4697620480 | bytes 12530692 | tf_op jit(solution)/shard_map/pallas_call | solution.py:380
  30.1 9.1 %shard_map.152 = (bf16[112,2048]{1,0:T(8,128)(2,1)S(1)}, bf16[112,4096]{1,0:T(8,128)(2,1)S(1)}, bf16[16,128]{1,0:T(8,128)(2,1)}) custom-call(s32[1]{0:T(128)} %bitcast.position, s32[128]{0:T(128)S(1)} %copy-done.9, s32[128]{0:T(128)S(1)} %copy-done.10, s32[2,256,1]{2,1,0:T(8,128)S(1)} %copy-done.11, s32[2,1,256]{2,1,0:T(1,128)S(1)} %copy-done.13, ...), custom_call_target="tpu_custom_call" | custom-call | flops 4697620480 | bytes 12076036 | tf_op jit(solution)/shard_map/pallas_call | solution.py:380
  39.2 3.5 %collective-permute-start.2 = (bf16[112,2048]{1,0:T(8,128)(2,1)S(1)}, bf16[112,2048]{1,0:T(8,128)(2,1)S(1)}, u32[]{:S(2)}, u32[]{:S(2)}) collective-permute-start(bf16[112,2048]{1,0:T(8,128)(2,1)S(1)} %get-tuple-element.32), channel_id=1, source_target_pairs={{0,1},{1,0},{2,3},{3,2},{4,5},{5,4},{6,7},{7,6},{8,9},{9,8},{10,11... | collective-permute-start | bytes 1376264 | tf_op jit(solution)/shard_map/ppermute | solution.py:450
  42.7 0.0 collective-permute-start.3
  42.7 2.8 %shard_map.153.own = bf16[224,2048]{1,0:T(8,128)(2,1)S(1)} custom-call(bf16[112,2048]{1,0:T(8,128)(2,1)S(1)} %get-tuple-element.20.own_rows.rows_same, bf16[112,2048]{1,0:T(8,128)(2,1)S(1)} %get-tuple-element.21.own_rows.rows_cross, bf16[112,4096]{1,0:T(8,128)(2,1)S(1)} %get-tuple-element.30.moves_same, bf16[112,4096]{1,0:T(8,128)(2,1)S(1)} %get-tuple-element.31.moves_cross, ...), custom_call_target="tpu_custom_call" | custom-call | flops 1879048192 | bytes 12062720 | tf_op jit(solution)/shard_map/pallas_call | solution.py:380
  45.5 0.0 collective-permute-done.2.far_same
  45.5 10.0 %collective-permute-done.3.far_cross = bf16[112,2048]{1,0:T(8,128)(2,1)S(1)} collective-permute-done((bf16[112,2048]{1,0:T(8,128)(2,1)S(1)}, bf16[112,2048]{1,0:T(8,128)(2,1)S(1)}, u32[]{:S(2)}, u32[]{:S(2)}) %collective-permute-start.3) | collective-permute-done | bytes 458784 | tf_op jit(solution)/shard_map/ppermute | solution.py:448
  55.5 1.8 %shard_map.154 = (bf16[392,1024]{1,0:T(8,128)(2,1)}, bf16[392,1024]{1,0:T(8,128)(2,1)}) custom-call(s32[1]{0:T(128)} %bitcast.position, s32[2,1,448]{2,1,0:T(1,128)S(1)} %copy-done.12, bf16[224,2048]{1,0:T(8,128)(2,1)S(1)} %shard_map.153.own, bf16[112,2048]{1,0:T(8,128)(2,1)S(1)} %collective-permute-done.2.far_same, ...), custom_call_target="tpu_custom_call" | custom-call | flops 719323136 | bytes 3444228 | tf_op jit(solution)/shard_map/pallas_call | solution.py:380
  (18 shorter events, 0.0 us)
Async XLA Ops:
  0.6 1.1 %copy-start.3 = (bf16[392,1024]{1,0:T(8,128)(2,1)S(1)}, bf16[392,1024]{1,0:T(8,128)(2,1)}, u32[]{:S(2)}) copy-start(bf16[392,1024]{1,0:T(8,128)(2,1)} %inputs.1) | copy-start | bytes 2408452
  1.8 1.1 %copy-start.4 = (bf16[392,1024]{1,0:T(8,128)(2,1)S(1)}, bf16[392,1024]{1,0:T(8,128)(2,1)}, u32[]{:S(2)}) copy-start(bf16[392,1024]{1,0:T(8,128)(2,1)} %out_grad.1) | copy-start | bytes 2408452
  2.9 0.9 %copy-start.6 = (s32[2,224,1]{2,1,0:T(8,128)S(1)}, s32[2,224,1]{2,1,0:T(8,128)}, u32[]{:S(2)}) copy-start(s32[2,224,1]{2,1,0:T(8,128)} %constant.15.clone.table) | copy-start | bytes 5380
  4.9 14.5 %collective-permute-start = (bf16[112,2048]{1,0:T(8,128)(2,1)S(1)}, bf16[112,2048]{1,0:T(8,128)(2,1)S(1)}, u32[]{:S(2)}, u32[]{:S(2)}) collective-permute-start(bf16[112,2048]{1,0:T(8,128)(2,1)S(1)} %get-tuple-element.23), channel_id=1, source_target_pairs={{0,1},{1,0},{2,3},{3,2},{4,5},{5,4},{6,7},{7,6},{8,9},{9,8},{10,11... | collective-permute-start | bytes 1376264 | tf_op jit(solution)/shard_map/ppermute | solution.py:415
  5.0 14.5 %collective-permute-start.1 = (bf16[112,2048]{1,0:T(8,128)(2,1)S(1)}, bf16[112,2048]{1,0:T(8,128)(2,1)S(1)}, u32[]{:S(2)}, u32[]{:S(2)}) collective-permute-start(bf16[112,2048]{1,0:T(8,128)(2,1)S(1)} %get-tuple-element.25), channel_id=1, source_target_pairs={{0,15},{1,2},{2,1},{3,4},{4,3},{5,6},{6,5},{7,8},{8,7},{9,10},{10,... | collective-permute-start | bytes 1376264 | tf_op jit(solution)/shard_map/ppermute | solution.py:414
  7.7 2.2 %copy-start = (bf16[1024,2048]{1,0:T(8,128)(2,1)S(1)}, bf16[1024,2048]{1,0:T(8,128)(2,1)}, u32[]{:S(2)}) copy-start(bf16[1024,2048]{1,0:T(8,128)(2,1)} %w_key_value.1) | copy-start | bytes 12582916
  9.9 1.6 %copy-start.1 = (bf16[1024,1024]{1,0:T(8,128)(2,1)S(1)}, bf16[1024,1024]{1,0:T(8,128)(2,1)}, u32[]{:S(2)}) copy-start(bf16[1024,1024]{1,0:T(8,128)(2,1)} %w_query.1) | copy-start | bytes 6291460
  11.5 1.6 %copy-start.2 = (bf16[1024,1024]{1,0:T(8,128)(2,1)S(1)}, bf16[1024,1024]{1,0:T(8,128)(2,1)}, u32[]{:S(2)}) copy-start(bf16[1024,1024]{1,0:T(8,128)(2,1)} %w_out.1) | copy-start | bytes 6291460
  13.1 0.9 %copy-start.5 = (s32[2,224,1]{2,1,0:T(8,128)S(1)}, s32[2,224,1]{2,1,0:T(8,128)}, u32[]{:S(2)}) copy-start(s32[2,224,1]{2,1,0:T(8,128)} %constant.14.clone.table) | copy-start | bytes 5380
  14.0 0.7 %copy-start.7 = (f32[1024]{0:T(1024)S(1)}, f32[1024]{0:T(1024)}, u32[]{:S(2)}) copy-start(f32[1024]{0:T(1024)} %param.18) | copy-start | bytes 12292
  14.7 0.7 %copy-start.8 = (f32[1024]{0:T(1024)S(1)}, f32[1024]{0:T(1024)}, u32[]{:S(2)}) copy-start(f32[1024]{0:T(1024)} %param.19) | copy-start | bytes 12292
  15.4 4.1 %copy-start.9 = (s32[128]{0:T(128)S(1)}, s32[128]{0:T(128)}, u32[]{:S(2)}) copy-start(s32[128]{0:T(128)} %live_rows.3) | copy-start | bytes 1540
  15.4 4.1 %copy-start.10 = (s32[128]{0:T(128)S(1)}, s32[128]{0:T(128)}, u32[]{:S(2)}) copy-start(s32[128]{0:T(128)} %live_cols.3) | copy-start | bytes 1540
  15.4 4.1 %copy-start.11 = (s32[2,256,1]{2,1,0:T(8,128)S(1)}, s32[2,256,1]{2,1,0:T(8,128)}, u32[]{:S(2)}) copy-start(s32[2,256,1]{2,1,0:T(8,128)} %constant.17.clone.code_column) | copy-start | bytes 6148
  15.4 4.2 %copy-start.13 = (s32[2,1,256]{2,1,0:T(1,128)S(1)}, s32[2,1,256]{2,1,0:T(1,128)}, u32[]{:S(2)}) copy-start(s32[2,1,256]{2,1,0:T(1,128)} %constant.18.clone.code_row) | copy-start | bytes 6148
  39.2 6.3 %collective-permute-start.2 = (bf16[112,2048]{1,0:T(8,128)(2,1)S(1)}, bf16[112,2048]{1,0:T(8,128)(2,1)S(1)}, u32[]{:S(2)}, u32[]{:S(2)}) collective-permute-start(bf16[112,2048]{1,0:T(8,128)(2,1)S(1)} %get-tuple-element.32), channel_id=1, source_target_pairs={{0,1},{1,0},{2,3},{3,2},{4,5},{5,4},{6,7},{7,6},{8,9},{9,8},{10,11... | collective-permute-start | bytes 1376264 | tf_op jit(solution)/shard_map/ppermute | solution.py:450
  42.7 12.8 %collective-permute-start.3 = (bf16[112,2048]{1,0:T(8,128)(2,1)S(1)}, bf16[112,2048]{1,0:T(8,128)(2,1)S(1)}, u32[]{:S(2)}, u32[]{:S(2)}) collective-permute-start(bf16[112,2048]{1,0:T(8,128)(2,1)S(1)} %get-tuple-element.33), channel_id=1, source_target_pairs={{0,15},{1,2},{2,1},{3,4},{4,3},{5,6},{6,5},{7,8},{8,7},{9,10},{10,... | collective-permute-start | bytes 1376264 | tf_op jit(solution)/shard_map/ppermute | solution.py:448
  42.7 12.8 %copy-start.12 = (s32[2,1,448]{2,1,0:T(1,128)S(1)}, s32[2,1,448]{2,1,0:T(1,128)}, u32[]{:S(2)}) copy-start(s32[2,1,448]{2,1,0:T(1,128)} %constant.16.clone.table) | copy-start | bytes 10756

commit v2 on v1

--- a/solution.py
+++ b/solution.py
@@ -7,6 +7,7 @@
 from jax.experimental import pallas as pl
 from jax.experimental.pallas import tpu as pltpu
 from jax.sharding import PartitionSpec as P
+
 
 HEAD_DIM = 32
 WT = 8
@@ -95,21 +96,23 @@
     return 1 - parity if kind == "same" else parity
 
 
-def pack_kernel(position, table, inputs, out_grad, same, cross, values, grads, sems):
+def pack_kernel(
+    position, send_table, own_table, inputs, out_grad, same, cross, values, grads, own_rows, send_rows, sems
+):
     width = inputs.shape[1]
-    copies = [
-        pltpu.make_async_copy(source, target, sems.at[place])
-        for place, (source, target) in enumerate(((inputs, values), (out_grad, grads)))
-    ]
+    moves = ((send_table, send_rows), (inputs, values), (out_grad, grads), (own_table, own_rows))
+    copies = [pltpu.make_async_copy(source, target, sems.at[place]) for place, (source, target) in enumerate(moves)]
     for copy in copies:
         copy.start()
-    one_hot = one_hot_rows(table[lax.rem(position[0], 2)], inputs.shape[0])
+    copies[0].wait()
+    one_hot = one_hot_rows(send_rows[lax.rem(position[0], 2)], inputs.shape[0])
     for place, source in enumerate((values, grads)):
-        copies[place].wait()
+        copies[1 + place].wait()
         rows = picked(one_hot, source[...])
         columns = slice(place * width, (place + 1) * width)
         same[:, columns] = rows[:ROWS]
         cross[:, columns] = rows[ROWS:]
+    copies[3].wait()
 
 
 def hidden_of(values, gain, bias):
@@ -118,35 +121,37 @@
 
 
 def own_kernel(
-    position, table, inputs, out_grad, gain, bias, w_query, w_key_value, w_out,
-    rows_same, rows_cross, heads_same, heads_cross, query_copy, pair_copy, out_copy, sems,
+    position, table, inputs, out_grad, w_query, w_key_value, w_out, gain, bias, code_column, code_row, unpack_table,
+    rows_same, rows_cross, heads_same, heads_cross, query_copy, pair_copy, out_copy, gain_copy, bias_copy,
+    column_copy, row_copy, unpack_copy, sems,
 ):
     width = inputs.shape[1]
     halves = [pl.ds(part * width, width) for part in range(2)]
-    copies = [pltpu.make_async_copy(w_query, query_copy, sems.at[0])]
-    copies += [
-        pltpu.make_async_copy(w_key_value.at[:, part], pair_copy.at[:, part], sems.at[1 + index])
-        for index, part in enumerate(halves)
-    ]
-    copies += [pltpu.make_async_copy(w_out, out_copy, sems.at[3])]
+    moves = [(gain, gain_copy), (bias, bias_copy), (w_query, query_copy)]
+    moves += [(w_key_value.at[:, part], pair_copy.at[:, part]) for part in halves]
+    moves += [(w_out, out_copy), (code_column, column_copy), (code_row, row_copy), (unpack_table, unpack_copy)]
+    copies = [pltpu.make_async_copy(source, target, sems.at[place]) for place, (source, target) in enumerate(moves)]
     for copy in copies:
         copy.start()
     one_hot = one_hot_rows(table[lax.rem(position[0], 2)], inputs.shape[0])
     values = picked(one_hot, inputs[...])
-    hidden = hidden_of(values, gain, bias)
+    copies[0].wait()
+    copies[1].wait()
+    hidden = hidden_of(values, gain_copy, bias_copy)
     grads = picked(one_hot, out_grad[...])
     for place, rows in enumerate((values, grads)):
         columns = slice(place * width, (place + 1) * width)
         rows_same[:, columns] = rows[:ROWS]
         rows_cross[:, columns] = rows[ROWS:]
     for part in range(3):
-        copies[part].wait()
+        copies[2 + part].wait()
         weights = query_copy[...] if part == 0 else pair_copy[:, halves[part - 1]]
         result = jnp.dot(hidden, weights, preferred_element_type=F32).astype(BF16)
         columns = slice(part * width, (part + 1) * width)
         heads_same[:, columns] = result[:ROWS]
         heads_cross[:, columns] = result[ROWS:]
-    copies[3].wait()
+    for copy in copies[5:]:
+        copy.wait()
 
 
 def cell_codes(slots, place, frames):
@@ -239,8 +244,8 @@
 
 
 def window_kernel(
-    kind, position, live_rows, live_cols, code_column, code_row, own_rows, own_heads, far_rows, other_far,
-    gain, bias, w_query, w_key_value, w_out, far_result, own_moves, other_heads,
+    kind, position, live_rows, live_cols, code_column, code_row, own_rows, own_heads, far_rows,
+    gain, bias, w_query, w_key_value, w_out, far_result, own_moves,
     heads, window_grads, grads_t, results, bias_of, query_t0, query_t1, *stages,
 ):
     width = far_rows.shape[1] // 2
@@ -275,17 +280,10 @@
 
     for block in range(groups):
         heads[block, WINDOW_ROWS:] = jnp.zeros((PADDED_ROWS - WINDOW_ROWS, GROUP_LANES), BF16)
-    if kind == "cross":
-        hidden = hidden_of(jnp.concatenate([far_rows[:, :width], other_far[:, :width]], axis=0), gain, bias)
+    hidden = hidden_of(far_rows[:, :width], gain, bias)
     for part in range(3):
-        columns = slice(part * width, (part + 1) * width)
-        if kind == "cross":
-            weights = w_query[...] if part == 0 else w_key_value[:, slice((part - 1) * width, part * width)]
-            result = jnp.dot(hidden, weights, preferred_element_type=F32).astype(BF16)
-            far = result[:ROWS]
-            other_heads[:, columns] = result[ROWS:]
-        else:
-            far = other_far[:, columns]
+        weights = w_query[...] if part == 0 else w_key_value[:, slice((part - 1) * width, part * width)]
+        far = jnp.dot(hidden, weights, preferred_element_type=F32).astype(BF16)
         for group in range(groups):
             lanes = slice(group * GROUP_LANES, (group + 1) * GROUP_LANES)
             first = part * width + group * GROUP_LANES
@@ -320,7 +318,7 @@
         softmax(1)
         return carry
 
-    lax.fori_loop(0, groups, body, 0)
+    lax.fori_loop(0, groups, body, 0, unroll=4)
     product(1, groups - 1)
 
     def rows_of(first, last):
@@ -333,21 +331,28 @@
         )
 
     own_moves[...] = rows_of((0, cut), (FIRST, second))
-    block_output, input_grad = finish(
-        far_rows[:, :width], far_rows[:, width:], rows_of((cut, FIRST), (second, WINDOW_ROWS)),
-        gain, w_query, w_key_value, w_out,
-    )
-    far_result[:, :width] = block_output
-    far_result[:, width:] = input_grad
-
-
-def tail_kernel(rows_same, rows_cross, moves_same, moves_cross, gain, w_query, w_key_value, w_out, out):
-    width = rows_same.shape[1] // 2
-    rows = jnp.concatenate([rows_same[...], rows_cross[...]], axis=0)
-    moves = jnp.concatenate([moves_same[...], moves_cross[...]], axis=0)
+    far_moves = rows_of((cut, FIRST), (second, WINDOW_ROWS))
+    if kind == "same":
+        far_result[...] = far_moves
+    else:
+        store_tail(far_result, far_rows[...], far_moves, gain, w_query, w_key_value, w_out)
+
+
+def store_tail(out, rows, moves, gain, w_query, w_key_value, w_out):
+    width = rows.shape[1] // 2
     block_output, input_grad = finish(rows[:, :width], rows[:, width:], moves, gain, w_query, w_key_value, w_out)
     out[:, :width] = block_output
     out[:, width:] = input_grad
+
+
+def tail_kernel(count, *refs):
+    rows, moves, weights, out = refs[:count], refs[count : 2 * count], refs[2 * count : -1], refs[-1]
+    rows = jnp.concatenate([x[...] for x in rows], axis=0)
+    moves = jnp.concatenate([x[...] for x in moves], axis=0)
+    store_tail(out, rows, moves, *weights)
+
+
+SMEM, VMEM, HBM = pltpu.SMEM, pltpu.VMEM, pltpu.HBM
 
 
 def unpack_kernel(position, table, own, far_same, far_cross, block_output, input_grad, outputs, sems):
@@ -374,53 +379,70 @@
 
 def call(kernel, outs, *operands, scratch=(), flops=0, megabytes=24):
     spaces, operands = zip(*operands)
-    out_spaces, shapes = zip(*outs)
-    outs = [jax.ShapeDtypeStruct(shape, BF16) for shape in shapes]
-    moved = sum(x.size * x.dtype.itemsize for x in operands) + sum(x.size * 2 for x in outs)
+    operands = [pltpu.with_memory_space_constraint(x, HBM) if s == HBM else x for s, x in zip(spaces, operands)]
+    outs = [out if len(out) == 3 else (*out, BF16) for out in outs]
+    shapes = [jax.ShapeDtypeStruct(shape, kind) for _, shape, kind in outs]
+    moved = sum(x.size * x.dtype.itemsize for x in operands) + sum(x.size * 2 for x in shapes)
     return pl.pallas_call(
         kernel,
-        out_shape=outs,
+        out_shape=shapes,
         in_specs=[pl.BlockSpec(memory_space=space) for space in spaces],
-        out_specs=[pl.BlockSpec(memory_space=space) for space in out_spaces],
+        out_specs=[pl.BlockSpec(memory_space=out[0]) for out in outs],
         scratch_shapes=list(scratch),
         compiler_params=pltpu.CompilerParams(vmem_limit_bytes=megabytes << 20),
         cost_estimate=pl.CostEstimate(flops=flops, bytes_accessed=moved, transcendentals=0),
     )(*operands)
 
 
-def on_device(inputs, out_grad, live_rows, live_cols, norm_gain, norm_bias, w_query, w_key_value, w_out):
+def vmem(*arrays):
+    return [(VMEM, x) for x in arrays]
+
+
+def hbm(*arrays):
+    return [(HBM, x) for x in arrays]
+
+
+def like(*arrays):
+    return [(VMEM, x.shape, x.dtype) for x in arrays]
+
+
+def staged(inputs, out_grad, live_rows, live_cols, norm_gain, norm_bias, w_query, w_key_value, w_out):
     token_count, width = inputs.shape
     groups = width // GROUP_LANES
     count = lax.axis_size("seq")
     position = (SMEM, lax.axis_index("seq").reshape(1))
     live = ((SMEM, live_rows), (SMEM, live_cols))
-    norm = ((VMEM, norm_gain.reshape(1, width)), (VMEM, norm_bias.reshape(1, width)))
-    own_table, send_table = (VMEM, jnp.asarray(OWN_TOKENS[..., None])), (VMEM, jnp.asarray(SEND_TOKENS[..., None]))
-    unpack_table = (VMEM, jnp.asarray(np.concatenate([OWN_TOKENS, SEND_TOKENS], axis=1)[:, None, :]))
-    codes = (VMEM, jnp.asarray(WINDOW_CODES[..., None])), (VMEM, jnp.asarray(WINDOW_CODES[:, None, :]))
+    own_table, send_table = jnp.asarray(OWN_TOKENS[..., None]), jnp.asarray(SEND_TOKENS[..., None])
+    unpack_table = jnp.asarray(np.concatenate([OWN_TOKENS, SEND_TOKENS], axis=1)[:, None, :])
+    constants = [
+        w_query, w_key_value, w_out, norm_gain.reshape(1, width), norm_bias.reshape(1, width),
+        jnp.asarray(WINDOW_CODES[..., None]), jnp.asarray(WINDOW_CODES[:, None, :]), unpack_table,
+    ]
 
     pair = [(i, i ^ 1) for i in range(count)]
     across = [(i, (i + 1) % count if i % 2 else (i - 1) % count) for i in range(count)]
 
     rows_out, heads_out, moves_out = (VMEM, (ROWS, 2 * width)), (VMEM, (ROWS, 3 * width)), (VMEM, (ROWS, 4 * width))
     product = 2 * width * width
-    send_same, send_cross, values, grads = call(
+    dma = pltpu.SemaphoreType.DMA
+    send_same, send_cross, values, grads, own_table = call(
         pack_kernel,
-        [rows_out] * 2 + [(VMEM, inputs.shape)] * 2,
-        position, send_table, (HBM, inputs), (HBM, out_grad),
-        scratch=[pltpu.SemaphoreType.DMA((2,))],
+        [rows_out] * 2 + like(inputs, out_grad, own_table),
+        position, *hbm(send_table, own_table, inputs, out_grad),
+        scratch=[VMEM(send_table.shape, send_table.dtype), dma((4,))],
         flops=4 * ROWS * token_count * 2 * width,
     )
     far_cross_rows = lax.ppermute(send_cross, "seq", across)
     far_same_rows = lax.ppermute(send_same, "seq", pair)
-    own_same_rows, own_cross_rows, own_same_heads, own_cross_heads, *weights = call(
+    own_same_rows, own_cross_rows, own_same_heads, own_cross_heads, *rest = call(
         own_kernel,
-        [rows_out] * 2 + [heads_out] * 2 + [(VMEM, w.shape) for w in (w_query, w_key_value, w_out)],
-        position, own_table, (VMEM, values), (VMEM, grads), *norm, (HBM, w_query), (HBM, w_key_value), (HBM, w_out),
-        scratch=[pltpu.SemaphoreType.DMA((4,))],
+        [rows_out] * 2 + [heads_out] * 2 + like(*constants),
+        position, *vmem(own_table, values, grads), *hbm(*constants),
+        scratch=[dma((9,))],
         flops=2 * ROWS * 4 * product,
     )
-    weights = [(VMEM, w) for w in weights]
+    w_query, w_key_value, w_out, gain, bias, code_column, code_row, unpack_table = rest
+    weights = vmem(w_query, w_key_value, w_out)
 
     stages = [VMEM((HEADS_PER_GROUP, n, GROUP_LANES), kind) for kind in (F32, F32, BF16, BF16) for n in (FIRST, SECOND)]
     scratch = [
@@ -434,29 +456,30 @@
         *stages,
     ]
 
-    def window(kind, own_rows, own_heads, far_rows, other_far):
-        outs = [rows_out, moves_out, heads_out if kind == "cross" else (VMEM, (16, GROUP_LANES))]
-        arrays = [(VMEM, x) for x in (own_rows, own_heads, far_rows, other_far)]
+    def window(kind, own_rows, own_heads, far_rows):
         return call(
-            functools.partial(window_kernel, kind), outs, position, *live, *codes, *arrays, *norm, *weights,
+            functools.partial(window_kernel, kind), [moves_out if kind == "same" else rows_out, moves_out],
+            position, *live, *vmem(code_column, code_row, own_rows, own_heads, far_rows, gain, bias), *weights,
             scratch=scratch, flops=2 * ROWS * 10 * product,
         )
 
-    far_cross, own_cross_moves, far_same_heads = window(
-        "cross", own_cross_rows, own_cross_heads, far_cross_rows, far_same_rows
-    )
+    def tail(rows, moves):
+        return call(
+            functools.partial(tail_kernel, len(rows)), [(VMEM, (len(rows) * ROWS, 2 * width))],
+            *vmem(*rows, *moves, gain), *weights, flops=len(rows) * ROWS * 4 * product,
+        )[0]
+
+    far_same_moves, own_same_moves = window("same", own_same_rows, own_same_heads, far_same_rows)
+    far_cross, own_cross_moves = window("cross", own_cross_rows, own_cross_heads, far_cross_rows)
     back_cross = lax.ppermute(far_cross, "seq", across)
-    far_same, own_same_moves, _ = window("same", own_same_rows, own_same_heads, far_same_rows, far_same_heads)
+    far_same = tail([far_same_rows], [far_same_moves])
     back_same = lax.ppermute(far_same, "seq", pair)
-    arrays = [(VMEM, x) for x in (own_same_rows, own_cross_rows, own_same_moves, own_cross_moves)]
-    (own,) = call(
-        tail_kernel, [(VMEM, (2 * ROWS, 2 * width))], *arrays, norm[0], *weights, flops=2 * ROWS * 4 * product
-    )
-    arrays = [(VMEM, x) for x in (own, back_same, back_cross)]
+    own = tail([own_same_rows, own_cross_rows], [own_same_moves, own_cross_moves])
     return tuple(
         call(
-            unpack_kernel, [(HBM, (token_count, width))] * 2, position, unpack_table, *arrays,
-            scratch=[VMEM((4, token_count, width // 2), BF16), pltpu.SemaphoreType.DMA((4,))],
+            unpack_kernel, [(HBM, (token_count, width))] * 2, position,
+            *vmem(unpack_table, own, back_same, back_cross),
+            scratch=[VMEM((4, token_count, width // 2), BF16), dma((4,))],
             flops=8 * ROWS * token_count * 2 * width,
         )
     )
@@ -465,4 +488,4 @@
 def solution(mesh):
     rows = P(("group", "seq"), None)
     in_specs = (rows, rows, P("group"), P("group"), P(), P(), P(), P(), P())
-    return jax.shard_map(on_device, mesh=mesh, in_specs=in_specs, out_specs=(rows, rows), check_vma=False)
+    return jax.shard_map(staged, mesh=mesh, in_specs=in_specs, out_specs=(rows, rows), check_vma=False)

time: 57.9 us -> 45.9 us (0.79)
  local copies, waits for them, and re-layouts: 10.9 us -> 0.01 us
  Pallas kernels: 29.3 us -> 28.5 us
    unnamed x28 -> x4, local copies, waits for them, and re-layouts: 10.9 us -> 0.01 us
    pallas_call x6 -> x7, Pallas kernels: 29.3 us -> 28.5 us  [call(): pl.pallas_call(kernel, out_shape=shapes, in_specs=[pl.BlockSpec(memory_sp...]
  transfers between devices with their start and end apart: 4 -> 4, of which waited for: 1 -> 1; matrix products, arithmetic and copies ran while one was open for 0% -> 0% of each run, Pallas kernels for 12% -> 54%
where the time goes in v2:
time: 45.9 us; the launch traced here: 45.8 us
  Pallas kernels  28.5 us (62%)
  waiting for transfers between devices  10 us (22%)
  starting transfers between devices  6.33 us (14%)
  between operations  0.88 us (2%)
    pallas_call x7, Pallas kernels, call(): pl.pallas_call(kernel, out_shape=shapes, in_specs=[pl.BlockSpec(memory_sp...  28.5 us
    ppermute x1, waiting for transfers between devices, staged(): back_cross = lax.ppermute(far_cross, 'seq', across)  10 us
    ppermute x1, starting transfers between devices, staged(): back_same = lax.ppermute(far_same, 'seq', pair)  3.54 us
    ppermute x1, starting transfers between devices, staged(): far_cross_rows = lax.ppermute(send_cross, 'seq', across)  2.63 us
  transfers between devices with their start and end apart: 4, of which 1 were waited for; matrix products, arithmetic and copies ran while one was open for 0% of the time, Pallas kernels for 54%

profile of v2, /device:TPU:1, one launch (start us, length us, event | category | flops | bytes accessed | tf_op | source)
XLA Modules:
  0.0 45.8 jit_solution(2153313125349983850)
XLA Ops:
  0.6 2.1 %shard_map.149 = (bf16[112,2048]{1,0:T(8,128)(2,1)S(1)}, bf16[112,2048]{1,0:T(8,128)(2,1)S(1)}, bf16[392,1024]{1,0:T(8,128)(2,1)S(1)}, bf16[392,1024]{1,0:T(8,128)(2,1)S(1)}, s32[2,224,1]{2,1,0:T(8,128)S(1)}) custom-call(s32[1]{0:T(128)} %bitcast.position, s32[2,224,1]{2,1,0:T(8,128)} %constant.15.clone.send_table, s32[2,224,1]{2,1,0:T(8,128)} %constant.14.clone.own_table, ...), custom_call_target="tpu_custom_call" | custom-call | flops 359661568 | bytes 4133252 | tf_op jit(solution)/shard_map/pallas_call | solution.py:386
  2.8 0.1 collective-permute-start
  2.9 2.6 %collective-permute-start.1 = (bf16[112,2048]{1,0:T(8,128)(2,1)S(1)}, bf16[112,2048]{1,0:T(8,128)(2,1)S(1)}, u32[]{:S(2)}, u32[]{:S(2)}) collective-permute-start(bf16[112,2048]{1,0:T(8,128)(2,1)S(1)} %get-tuple-element.40), channel_id=1, source_target_pairs={{0,15},{1,2},{2,1},{3,4},{4,3},{5,6},{6,5},{7,8},{8,7},{9,10},{10,... | collective-permute-start | bytes 1376264 | tf_op jit(solution)/shard_map/ppermute | solution.py:435
  5.5 0.0 copy-start
  5.5 0.0 copy-start.1
  5.5 3.7 %shard_map.150 = (bf16[112,2048]{1,0:T(8,128)(2,1)S(1)}, bf16[112,2048]{1,0:T(8,128)(2,1)S(1)}, bf16[112,3072]{1,0:T(8,128)(2,1)S(1)}, bf16[112,3072]{1,0:T(8,12...) custom-call(s32[1]{0:T(128)} %bitcast.position, ...), custom_call_target="tpu_custom_call" | custom-call | flops 1879048192 | bytes 20702212 | tf_op jit(solution)/shard_map/pallas_call | solution.py:386
  9.2 0.0 collective-permute-done.far_rows.refs_0_
  9.2 0.0 copy-done
  9.2 0.0 copy-done.1
  9.2 6.9 %shard_map.151 = (bf16[112,4096]{1,0:T(8,128)(2,1)S(1)}, bf16[112,4096]{1,0:T(8,128)(2,1)S(1)}) custom-call(s32[1]{0:T(128)} %bitcast.position, s32[128]{0:T(128)S(1)} %copy-done, s32[128]{0:T(128)S(1)} %copy-done.1, s32[2,256,1]{2,1,0:T(8,128)S(1)} %get-tuple-element.29.code_column, s32[2,1,256]{2,1,0:T(1,128)S(1)} %get-tuple-element.30.code_row, ...), custom_call_target="tpu_custom_call" | custom-call | flops 4697620480 | bytes 11842564 | tf_op jit(solution)/shard_map/pallas_call | solution.py:386
  16.2 2.3 %shard_map.154 = bf16[112,2048]{1,0:T(8,128)(2,1)S(1)} custom-call(bf16[112,2048]{1,0:T(8,128)(2,1)S(1)} %collective-permute-done.far_rows.refs_0_, bf16[112,4096]{1,0:T(8,128)(2,1)S(1)} %get-tuple-element.42.refs_1_, f32[1,1024]{1,0:T(1,128)S(1)} %get-tuple-element.33.gain.refs_4_.refs_2_, bf16[1024,1024]{1,0:T(8,128)(2,1)S(1)} %get-tuple-element.35.w_query.refs_5_.refs_3_, ...), custom_call_target="tpu_custom_call" | custom-call | flops 939524096 | bytes 10227712 | tf_op jit(solution)/shard_map/pallas_call | solution.py:386
  18.5 3.5 %collective-permute-start.2 = (bf16[112,2048]{1,0:T(8,128)(2,1)S(1)}, bf16[112,2048]{1,0:T(8,128)(2,1)S(1)}, u32[]{:S(2)}, u32[]{:S(2)}) collective-permute-start(bf16[112,2048]{1,0:T(8,128)(2,1)S(1)} %shard_map.154), channel_id=1, source_target_pairs={{0,1},{1,0},{2,3},{3,2},{4,5},{5,4},{6,7},{7,6},{8,9},{9,8},{10,11... | collective-permute-start | bytes 1376264 | tf_op jit(solution)/shard_map/ppermute | solution.py:476
  22.1 0.0 collective-permute-done.1.far_rows
  22.1 8.8 %shard_map.152 = (bf16[112,2048]{1,0:T(8,128)(2,1)S(1)}, bf16[112,4096]{1,0:T(8,128)(2,1)S(1)}) custom-call(s32[1]{0:T(128)} %bitcast.position, s32[128]{0:T(128)S(1)} %copy-done, s32[128]{0:T(128)S(1)} %copy-done.1, s32[2,256,1]{2,1,0:T(8,128)S(1)} %get-tuple-element.29.code_column, s32[2,1,256]{2,1,0:T(1,128)S(1)} %get-tuple-element.30.code_row, ...), custom_call_target="tpu_custom_call" | custom-call | flops 4697620480 | bytes 11383812 | tf_op jit(solution)/shard_map/pallas_call | solution.py:386
  30.9 0.1 collective-permute-start.3
  31.0 2.8 %shard_map.153.own = bf16[224,2048]{1,0:T(8,128)(2,1)S(1)} custom-call(bf16[112,2048]{1,0:T(8,128)(2,1)S(1)} %get-tuple-element.27.own_rows.refs_0_, bf16[112,2048]{1,0:T(8,128)(2,1)S(1)} %get-tuple-element.28.own_rows.refs_1_, bf16[112,4096]{1,0:T(8,128)(2,1)S(1)} %get-tuple-element.38.refs_2_, bf16[112,4096]{1,0:T(8,128)(2,1)S(1)} %get-tuple-element.41.refs_3_, ...), custom_call_target="tpu_custom_call" | custom-call | flops 1879048192 | bytes 12062720 | tf_op jit(solution)/shard_map/pallas_call | solution.py:386
  33.8 0.0 collective-permute-done.2.far_same
  33.8 10.0 %collective-permute-done.3.far_cross = bf16[112,2048]{1,0:T(8,128)(2,1)S(1)} collective-permute-done((bf16[112,2048]{1,0:T(8,128)(2,1)S(1)}, bf16[112,2048]{1,0:T(8,128)(2,1)S(1)}, u32[]{:S(2)}, u32[]{:S(2)}) %collective-permute-start.3) | collective-permute-done | bytes 458784 | tf_op jit(solution)/shard_map/ppermute | solution.py:474
  43.8 1.8 %shard_map.155 = (bf16[392,1024]{1,0:T(8,128)(2,1)}, bf16[392,1024]{1,0:T(8,128)(2,1)}) custom-call(s32[1]{0:T(128)} %bitcast.position, s32[2,1,448]{2,1,0:T(1,128)S(1)} %get-tuple-element.26.table, bf16[224,2048]{1,0:T(8,128)(2,1)S(1)} %shard_map.153.own, bf16[112,2048]{1,0:T(8,128)(2,1)S(1)} %collective-permute-done.2.far_same, ...), custom_call_target="tpu_custom_call" | custom-call | flops 719323136 | bytes 3444228 | tf_op jit(solution)/shard_map/pallas_call | solution.py:386
Async XLA Ops:
  2.8 6.4 %collective-permute-start = (bf16[112,2048]{1,0:T(8,128)(2,1)S(1)}, bf16[112,2048]{1,0:T(8,128)(2,1)S(1)}, u32[]{:S(2)}, u32[]{:S(2)}) collective-permute-start(bf16[112,2048]{1,0:T(8,128)(2,1)S(1)} %get-tuple-element.32), channel_id=1, source_target_pairs={{0,1},{1,0},{2,3},{3,2},{4,5},{5,4},{6,7},{7,6},{8,9},{9,8},{10,11... | collective-permute-start | bytes 1376264 | tf_op jit(solution)/shard_map/ppermute | solution.py:436
  2.9 19.2 %collective-permute-start.1 = (bf16[112,2048]{1,0:T(8,128)(2,1)S(1)}, bf16[112,2048]{1,0:T(8,128)(2,1)S(1)}, u32[]{:S(2)}, u32[]{:S(2)}) collective-permute-start(bf16[112,2048]{1,0:T(8,128)(2,1)S(1)} %get-tuple-element.40), channel_id=1, source_target_pairs={{0,15},{1,2},{2,1},{3,4},{4,3},{5,6},{6,5},{7,8},{8,7},{9,10},{10,... | collective-permute-start | bytes 1376264 | tf_op jit(solution)/shard_map/ppermute | solution.py:435
  5.5 3.7 %copy-start = (s32[128]{0:T(128)S(1)}, s32[128]{0:T(128)}, u32[]{:S(2)}) copy-start(s32[128]{0:T(128)} %live_rows.3) | copy-start | bytes 1540
  5.5 3.7 %copy-start.1 = (s32[128]{0:T(128)S(1)}, s32[128]{0:T(128)}, u32[]{:S(2)}) copy-start(s32[128]{0:T(128)} %live_cols.3) | copy-start | bytes 1540
  18.5 15.2 %collective-permute-start.2 = (bf16[112,2048]{1,0:T(8,128)(2,1)S(1)}, bf16[112,2048]{1,0:T(8,128)(2,1)S(1)}, u32[]{:S(2)}, u32[]{:S(2)}) collective-permute-start(bf16[112,2048]{1,0:T(8,128)(2,1)S(1)} %shard_map.154), channel_id=1, source_target_pairs={{0,1},{1,0},{2,3},{3,2},{4,5},{5,4},{6,7},{7,6},{8,9},{9,8},{10,11... | collective-permute-start | bytes 1376264 | tf_op jit(solution)/shard_map/ppermute | solution.py:476
  30.9 12.9 %collective-permute-start.3 = (bf16[112,2048]{1,0:T(8,128)(2,1)S(1)}, bf16[112,2048]{1,0:T(8,128)(2,1)S(1)}, u32[]{:S(2)}, u32[]{:S(2)}) collective-permute-start(bf16[112,2048]{1,0:T(8,128)(2,1)S(1)} %get-tuple-element.43), channel_id=1, source_target_pairs={{0,15},{1,2},{2,1},{3,4},{4,3},{5,6},{6,5},{7,8},{8,7},{9,10},{10,... | collective-permute-start | bytes 1376264 | tf_op jit(solution)/shard_map/ppermute | solution.py:474

commit v3 on v2

--- a/solution.py
+++ b/solution.py
@@ -227,27 +227,33 @@
     results[3 * groups + group, keys] = per_key(probs, grad)
 
 
-def finish(values, grads, results, gain, w_query, w_key_value, w_out):
-    width = values.shape[1]
-    rows = values.shape[0]
-    block_output = values.astype(F32) + jnp.dot(results[:, :width], w_out[...], preferred_element_type=F32)
-    fill = -rows % GROUP_LANES
-    moves = jnp.concatenate([results[:, width:], jnp.zeros((fill, 3 * width), BF16)], axis=0)
+def output_of(rows, context, w_out):
+    width = context.shape[1]
+    context_out = jnp.dot(context, w_out[...], preferred_element_type=F32)
+    return (rows[:, :width].astype(F32) + context_out).astype(BF16)
+
+
+def input_grad_of(rows, moves, gain, w_query, w_key_value):
+    count, width = rows.shape[0], rows.shape[1] // 2
+    fill = -count % GROUP_LANES
+    if fill:
+        moves = jnp.concatenate([moves, jnp.zeros((fill, 3 * width), BF16)], axis=0)
     grad_hidden = lax.dot_general(w_query[...], moves[:, :width], NT, preferred_element_type=F32)
     grad_hidden = grad_hidden + lax.dot_general(w_key_value[...], moves[:, width:], NT, preferred_element_type=F32)
-    grad_hidden = grad_hidden.T[:rows]
-    unit, inv_dev = normalized(values)
+    grad_hidden = grad_hidden.T[:count]
+    unit, inv_dev = normalized(rows[:, :width])
     scaled = grad_hidden * gain[...]
     centred = scaled - jnp.mean(scaled, axis=-1, keepdims=True)
     norm_grad = inv_dev * (centred - unit * jnp.mean(scaled * unit, axis=-1, keepdims=True))
-    return block_output.astype(BF16), (grads.astype(F32) + norm_grad).astype(BF16)
+    return (rows[:, width:].astype(F32) + norm_grad).astype(BF16)
 
 
 def window_kernel(
     kind, position, live_rows, live_cols, code_column, code_row, own_rows, own_heads, far_rows,
-    gain, bias, w_query, w_key_value, w_out, far_result, own_moves,
-    heads, window_grads, grads_t, results, bias_of, query_t0, query_t1, *stages,
+    gain, bias, w_query, w_key_value, w_out, own_moves, far_moves, *rest,
 ):
+    far_output, rest = (rest[:1], rest[1:]) if kind == "cross" else ((), rest)
+    heads, window_grads, grads_t, results, bias_of, query_t0, query_t1, *stages = rest
     width = far_rows.shape[1] // 2
     groups = width // GROUP_LANES
     cut, second = SLOTS[0], FIRST + SLOTS[1]
@@ -331,31 +337,38 @@
         )
 
     own_moves[...] = rows_of((0, cut), (FIRST, second))
-    far_moves = rows_of((cut, FIRST), (second, WINDOW_ROWS))
+    far_moved = rows_of((cut, FIRST), (second, WINDOW_ROWS))
     if kind == "same":
-        far_result[...] = far_moves
+        far_moves[...] = far_moved
     else:
-        store_tail(far_result, far_rows[...], far_moves, gain, w_query, w_key_value, w_out)
-
-
-def store_tail(out, rows, moves, gain, w_query, w_key_value, w_out):
-    width = rows.shape[1] // 2
-    block_output, input_grad = finish(rows[:, :width], rows[:, width:], moves, gain, w_query, w_key_value, w_out)
-    out[:, :width] = block_output
-    out[:, width:] = input_grad
-
-
-def tail_kernel(count, *refs):
-    rows, moves, weights, out = refs[:count], refs[count : 2 * count], refs[2 * count : -1], refs[-1]
-    rows = jnp.concatenate([x[...] for x in rows], axis=0)
-    moves = jnp.concatenate([x[...] for x in moves], axis=0)
-    store_tail(out, rows, moves, *weights)
+        far_moves[...] = far_moved[:, width:]
+        far_output[0][...] = output_of(far_rows[...], far_moved[:, :width], w_out)
+
+
+def far_tail_kernel(rows_same, rows_cross, moves_same, moves_cross, gain, w_query, w_key_value, w_out, same, cross):
+    width = cross.shape[1]
+    rows = jnp.concatenate([rows_same[...], rows_cross[...]], axis=0)
+    moves = jnp.concatenate([moves_same[:, width:], moves_cross[...]], axis=0)
+    input_grad = input_grad_of(rows, moves, gain, w_query, w_key_value)
+    cross[...] = input_grad[ROWS:]
+    same[:, width:] = input_grad[:ROWS]
+    same[:, :width] = output_of(rows_same[...], moves_same[:, :width], w_out)
+
+
+def own_tail_kernel(rows_same, rows_cross, moves_same, moves_cross, gain, w_query, w_key_value, w_out, out):
+    width = out.shape[1] // 2
+    rows = jnp.concatenate([rows_same[...], rows_cross[...]], axis=0)
+    moves = jnp.concatenate([moves_same[...], moves_cross[...]], axis=0)
+    out[:, :width] = output_of(rows, moves[:, :width], w_out)
+    out[:, width:] = input_grad_of(rows, moves[:, width:], gain, w_query, w_key_value)
 
 
 SMEM, VMEM, HBM = pltpu.SMEM, pltpu.VMEM, pltpu.HBM
 
 
-def unpack_kernel(position, table, own, far_same, far_cross, block_output, input_grad, outputs, sems):
+def unpack_kernel(
+    position, table, own, far_same, far_output, far_grad, block_output, input_grad, outputs, sems
+):
     width = block_output.shape[1]
     chunk = width // 2
     token = lax.broadcasted_iota(jnp.int32, (block_output.shape[0], 4 * ROWS), 0)
@@ -363,11 +376,13 @@
     copies = []
     for index in range(4):
         columns = slice(index * chunk, (index + 1) * chunk)
-        values = jnp.concatenate([own[:, columns], far_same[:, columns], far_cross[:, columns]], axis=0)
+        far_cross = far_output if index < 2 else far_grad
+        place = pl.ds(index % 2 * chunk, chunk)
+        values = jnp.concatenate([own[:, columns], far_same[:, columns], far_cross[:, place]], axis=0)
         outputs[index] = picked(one_hot, values)
         target = block_output if index < 2 else input_grad
         copies.append(
-            pltpu.make_async_copy(outputs.at[index], target.at[:, pl.ds(index % 2 * chunk, chunk)], sems.at[index])
+            pltpu.make_async_copy(outputs.at[index], target.at[:, place], sems.at[index])
         )
         copies[-1].start()
     for copy in copies:
@@ -456,29 +471,35 @@
         *stages,
     ]
 
+    half_out = (VMEM, (ROWS, width))
+
     def window(kind, own_rows, own_heads, far_rows):
         return call(
-            functools.partial(window_kernel, kind), [moves_out if kind == "same" else rows_out, moves_out],
+            functools.partial(window_kernel, kind),
+            [moves_out] * 2 if kind == "same" else [moves_out, heads_out, half_out],
             position, *live, *vmem(code_column, code_row, own_rows, own_heads, far_rows, gain, bias), *weights,
-            scratch=scratch, flops=2 * ROWS * 10 * product,
+            scratch=scratch, flops=2 * ROWS * 8 * product,
         )
 
-    def tail(rows, moves):
-        return call(
-            functools.partial(tail_kernel, len(rows)), [(VMEM, (len(rows) * ROWS, 2 * width))],
-            *vmem(*rows, *moves, gain), *weights, flops=len(rows) * ROWS * 4 * product,
-        )[0]
-
-    far_same_moves, own_same_moves = window("same", own_same_rows, own_same_heads, far_same_rows)
-    far_cross, own_cross_moves = window("cross", own_cross_rows, own_cross_heads, far_cross_rows)
-    back_cross = lax.ppermute(far_cross, "seq", across)
-    far_same = tail([far_same_rows], [far_same_moves])
+    own_same_moves, far_same_moves = window("same", own_same_rows, own_same_heads, far_same_rows)
+    own_cross_moves, far_cross_moves, far_output = window("cross", own_cross_rows, own_cross_heads, far_cross_rows)
+    back_output = lax.ppermute(far_output, "seq", across)
+    far_same, far_grad = call(
+        far_tail_kernel, [rows_out, half_out],
+        *vmem(far_same_rows, far_cross_rows, far_same_moves, far_cross_moves, gain), *weights,
+        flops=2 * ROWS * 4 * product,
+    )
+    back_grad = lax.ppermute(far_grad, "seq", across)
     back_same = lax.ppermute(far_same, "seq", pair)
-    own = tail([own_same_rows, own_cross_rows], [own_same_moves, own_cross_moves])
+    (own,) = call(
+        own_tail_kernel, [(VMEM, (2 * ROWS, 2 * width))],
+        *vmem(own_same_rows, own_cross_rows, own_same_moves, own_cross_moves, gain), *weights,
+        flops=2 * ROWS * 4 * product,
+    )
     return tuple(
         call(
             unpack_kernel, [(HBM, (token_count, width))] * 2, position,
-            *vmem(unpack_table, own, back_same, back_cross),
+            *vmem(unpack_table, own, back_same, back_output, back_grad),
             scratch=[VMEM((4, token_count, width // 2), BF16), dma((4,))],
             flops=8 * ROWS * token_count * 2 * width,
         )

time: 45.9 us -> 48.8 us (1.063)
  waiting for transfers between devices: 10 us -> 12.9 us
  Pallas kernels: 28.5 us -> 27 us
  starting transfers between devices: 6.33 us -> 7.48 us
    ppermute x1, waiting for transfers between devices: 0.01 us -> 4.48 us  [staged(): far_cross_rows = lax.ppermute(send_cross, 'seq', across)]
    ppermute x1, starting transfers between devices: 3.54 us -> 0.07 us  [staged(): back_same = lax.ppermute(far_same, 'seq', pair)]
    ppermute x1, starting transfers between devices: 0.09 us -> 2.89 us  [staged(): far_same_rows = lax.ppermute(send_same, 'seq', pair)]
    ppermute x1 -> x2, starting transfers between devices: 0.07 us -> 1.88 us  [the longest x1 1.8 us: staged(): back_output = lax.ppermute(far_output, 'seq', across)]
    ppermute x1 -> x2, waiting for transfers between devices: 10 us -> 8.38 us  [the longest x1 5.05 us: staged(): back_output = lax.ppermute(far_output, 'seq', across)]
    pallas_call x7, Pallas kernels: 28.5 us -> 27 us  [call(): pl.pallas_call(kernel, out_shape=shapes, in_specs=[pl.BlockSpec(memory_sp...]
  transfers between devices with their start and end apart: 4 -> 5, of which waited for: 1 -> 3; matrix products, arithmetic and copies ran while one was open for 0% -> 0% of each run, Pallas kernels for 54% -> 28%
where the time goes in v3:
time: 48.8 us; the launch traced here: 48.2 us
  Pallas kernels  27 us (55%)
  waiting for transfers between devices  12.9 us (26%)
  starting transfers between devices  7.48 us (15%)
  between operations  0.86 us (2%)
    pallas_call x7, Pallas kernels, call(): pl.pallas_call(kernel, out_shape=shapes, in_specs=[pl.BlockSpec(memory_sp...  27 us
    ppermute x1, waiting for transfers between devices, staged(): back_output = lax.ppermute(far_output, 'seq', across)  5.05 us
    ppermute x1, waiting for transfers between devices, staged(): far_cross_rows = lax.ppermute(send_cross, 'seq', across)  4.48 us
    ppermute x1, waiting for transfers between devices, staged(): back_grad = lax.ppermute(far_grad, 'seq', across)  3.34 us
    ppermute x1, starting transfers between devices, staged(): far_same_rows = lax.ppermute(send_same, 'seq', pair)  2.89 us
    ppermute x1, starting transfers between devices, staged(): far_cross_rows = lax.ppermute(send_cross, 'seq', across)  2.64 us
    ppermute x1, starting transfers between devices, staged(): back_output = lax.ppermute(far_output, 'seq', across)  1.8 us
  transfers between devices with their start and end apart: 5, of which 3 were waited for; matrix products, arithmetic and copies ran while one was open for 0% of the time, Pallas kernels for 28%

profile of v3, /device:TPU:1, one launch (start us, length us, event | category | flops | bytes accessed | tf_op | source)
XLA Modules:
  0.0 48.2 jit_solution(10525360980730139920)
XLA Ops:
  0.6 2.1 %shard_map.149 = (bf16[112,2048]{1,0:T(8,128)(2,1)S(1)}, bf16[112,2048]{1,0:T(8,128)(2,1)S(1)}, bf16[392,1024]{1,0:T(8,128)(2,1)S(1)}, bf16[392,1024]{1,0:T(8,128)(2,1)S(1)}, s32[2,224,1]{2,1,0:T(8,128)S(1)}) custom-call(s32[1]{0:T(128)} %bitcast.position, s32[2,224,1]{2,1,0:T(8,128)} %constant.15.clone.send_table, s32[2,224,1]{2,1,0:T(8,128)} %constant.14.clone.own_table, ...), custom_call_target="tpu_custom_call" | custom-call | flops 359661568 | bytes 4133252 | tf_op jit(solution)/shard_map/pallas_call | solution.py:401
  2.8 2.6 %collective-permute-start.1 = (bf16[112,2048]{1,0:T(8,128)(2,1)S(1)}, bf16[112,2048]{1,0:T(8,128)(2,1)S(1)}, u32[]{:S(2)}, u32[]{:S(2)}) collective-permute-start(bf16[112,2048]{1,0:T(8,128)(2,1)S(1)} %get-tuple-element.43), channel_id=1, source_target_pairs={{0,15},{1,2},{2,1},{3,4},{4,3},{5,6},{6,5},{7,8},{8,7},{9,10},{10,... | collective-permute-start | bytes 1376264 | tf_op jit(solution)/shard_map/ppermute | solution.py:450
  5.4 2.9 %collective-permute-start = (bf16[112,2048]{1,0:T(8,128)(2,1)S(1)}, bf16[112,2048]{1,0:T(8,128)(2,1)S(1)}, u32[]{:S(2)}, u32[]{:S(2)}) collective-permute-start(bf16[112,2048]{1,0:T(8,128)(2,1)S(1)} %get-tuple-element.35), channel_id=1, source_target_pairs={{0,1},{1,0},{2,3},{3,2},{4,5},{5,4},{6,7},{7,6},{8,9},{9,8},{10,11... | collective-permute-start | bytes 1376264 | tf_op jit(solution)/shard_map/ppermute | solution.py:451
  8.3 0.0 copy-start
  8.3 0.0 copy-start.1
  8.3 3.7 %shard_map.150 = (bf16[112,2048]{1,0:T(8,128)(2,1)S(1)}, bf16[112,2048]{1,0:T(8,128)(2,1)S(1)}, bf16[112,3072]{1,0:T(8,128)(2,1)S(1)}, bf16[112,3072]{1,0:T(8,12...) custom-call(s32[1]{0:T(128)} %bitcast.position, ...), custom_call_target="tpu_custom_call" | custom-call | flops 1879048192 | bytes 20702212 | tf_op jit(solution)/shard_map/pallas_call | solution.py:401
  12.0 4.5 %collective-permute-done.1.far_rows.rows_cross = bf16[112,2048]{1,0:T(8,128)(2,1)S(1)} collective-permute-done((bf16[112,2048]{1,0:T(8,128)(2,1)S(1)}, bf16[112,2048]{1,0:T(8,128)(2,1)S(1)}, u32[]{:S(2)}, u32[]{:S(2)}) %collective-permute-start.1) | collective-permute-done | bytes 458784 | tf_op jit(solution)/shard_map/ppermute | solution.py:450
  16.5 0.0 copy-done
  16.5 0.0 copy-done.1
  16.5 7.2 %shard_map.152 = (bf16[112,4096]{1,0:T(8,128)(2,1)S(1)}, bf16[112,3072]{1,0:T(8,128)(2,1)S(1)}, bf16[112,1024]{1,0:T(8,128)(2,1)S(1)}) custom-call(s32[1]{0:T(128)} %bitcast.position, s32[128]{0:T(128)S(1)} %copy-done, s32[128]{0:T(128)S(1)} %copy-done.1, s32[2,256,1]{2,1,0:T(8,128)S(1)} %get-tuple-element.32.code_column, ...), custom_call_target="tpu_custom_call" | custom-call | flops 3758096384 | bytes 11842564 | tf_op jit(solution)/shard_map/pallas_call | solution.py:401
  23.7 0.0 collective-permute-done.far_rows.rows_same
  23.7 6.7 %shard_map.151 = (bf16[112,4096]{1,0:T(8,128)(2,1)S(1)}, bf16[112,4096]{1,0:T(8,128)(2,1)S(1)}) custom-call(s32[1]{0:T(128)} %bitcast.position, s32[128]{0:T(128)S(1)} %copy-done, s32[128]{0:T(128)S(1)} %copy-done.1, s32[2,256,1]{2,1,0:T(8,128)S(1)} %get-tuple-element.32.code_column, s32[2,1,256]{2,1,0:T(1,128)S(1)} %get-tuple-element.33.code_row, ...), custom_call_target="tpu_custom_call" | custom-call | flops 3758096384 | bytes 11842564 | tf_op jit(solution)/shard_map/pallas_call | solution.py:401
  30.5 2.6 %shard_map.154 = (bf16[112,2048]{1,0:T(8,128)(2,1)S(1)}, bf16[112,1024]{1,0:T(8,128)(2,1)S(1)}) custom-call(bf16[112,2048]{1,0:T(8,128)(2,1)S(1)} %collective-permute-done.far_rows.rows_same, bf16[112,2048]{1,0:T(8,128)(2,1)S(1)} %collective-permute-done.1.far_rows.rows_cross, bf16[112,4096]{1,0:T(8,128)(2,1)S(1)} %get-tuple-element.45.moves_same, ...), custom_call_target="tpu_custom_call" | custom-call | flops 1879048192 | bytes 11603968 | tf_op jit(solution)/shard_map/pallas_call | solution.py:401
  33.1 0.1 collective-permute-start.2
  33.2 1.8 %collective-permute-start.3 = (bf16[112,1024]{1,0:T(8,128)(2,1)S(1)}, bf16[112,1024]{1,0:T(8,128)(2,1)S(1)}, u32[]{:S(2)}, u32[]{:S(2)}) collective-permute-start(bf16[112,1024]{1,0:T(8,128)(2,1)S(1)} %get-tuple-element.48), channel_id=1, source_target_pairs={{0,15},{1,2},{2,1},{3,4},{4,3},{5,6},{6,5},{7,8},{8,7},{9,10},{10,... | collective-permute-start | bytes 688136 | tf_op jit(solution)/shard_map/ppermute | solution.py:486
  35.0 0.1 collective-permute-start.4
  35.1 2.7 %shard_map.153.own = bf16[224,2048]{1,0:T(8,128)(2,1)S(1)} custom-call(bf16[112,2048]{1,0:T(8,128)(2,1)S(1)} %get-tuple-element.30.own_rows.rows_same, bf16[112,2048]{1,0:T(8,128)(2,1)S(1)} %get-tuple-element.31.own_rows.rows_cross, bf16[112,4096]{1,0:T(8,128)(2,1)S(1)} %get-tuple-element.41.moves_same, bf16[112,4096]{1,0:T(8,128)(2,1)S(1)} %get-tuple-element.44.moves_cross, ...), custom_call_target="tpu_custom_call" | custom-call | flops 1879048192 | bytes 12062720 | tf_op jit(solution)/shard_map/pallas_call | solution.py:401
  37.8 5.0 %collective-permute-done.3.far_output = bf16[112,1024]{1,0:T(8,128)(2,1)S(1)} collective-permute-done((bf16[112,1024]{1,0:T(8,128)(2,1)S(1)}, bf16[112,1024]{1,0:T(8,128)(2,1)S(1)}, u32[]{:S(2)}, u32[]{:S(2)}) %collective-permute-start.3) | collective-permute-done | bytes 229408 | tf_op jit(solution)/shard_map/ppermute | solution.py:486
  42.9 3.3 %collective-permute-done.4.far_grad = bf16[112,1024]{1,0:T(8,128)(2,1)S(1)} collective-permute-done((bf16[112,1024]{1,0:T(8,128)(2,1)S(1)}, bf16[112,1024]{1,0:T(8,128)(2,1)S(1)}, u32[]{:S(2)}, u32[]{:S(2)}) %collective-permute-start.4) | collective-permute-done | bytes 229408 | tf_op jit(solution)/shard_map/ppermute | solution.py:492
  46.2 0.0 collective-permute-done.2.far_same
  46.2 1.8 %shard_map.155 = (bf16[392,1024]{1,0:T(8,128)(2,1)}, bf16[392,1024]{1,0:T(8,128)(2,1)}) custom-call(s32[1]{0:T(128)} %bitcast.position, s32[2,1,448]{2,1,0:T(1,128)S(1)} %get-tuple-element.29.table, bf16[224,2048]{1,0:T(8,128)(2,1)S(1)} %shard_map.153.own, bf16[112,2048]{1,0:T(8,128)(2,1)S(1)} %collective-permute-done.2.far_same, ...), custom_call_target="tpu_custom_call" | custom-call | flops 719323136 | bytes 3444228 | tf_op jit(solution)/shard_map/pallas_call | solution.py:401
Async XLA Ops:
  2.8 13.7 %collective-permute-start.1 = (bf16[112,2048]{1,0:T(8,128)(2,1)S(1)}, bf16[112,2048]{1,0:T(8,128)(2,1)S(1)}, u32[]{:S(2)}, u32[]{:S(2)}) collective-permute-start(bf16[112,2048]{1,0:T(8,128)(2,1)S(1)} %get-tuple-element.43), channel_id=1, source_target_pairs={{0,15},{1,2},{2,1},{3,4},{4,3},{5,6},{6,5},{7,8},{8,7},{9,10},{10,... | collective-permute-start | bytes 1376264 | tf_op jit(solution)/shard_map/ppermute | solution.py:450
  5.4 18.3 %collective-permute-start = (bf16[112,2048]{1,0:T(8,128)(2,1)S(1)}, bf16[112,2048]{1,0:T(8,128)(2,1)S(1)}, u32[]{:S(2)}, u32[]{:S(2)}) collective-permute-start(bf16[112,2048]{1,0:T(8,128)(2,1)S(1)} %get-tuple-element.35), channel_id=1, source_target_pairs={{0,1},{1,0},{2,3},{3,2},{4,5},{5,4},{6,7},{7,6},{8,9},{9,8},{10,11... | collective-permute-start | bytes 1376264 | tf_op jit(solution)/shard_map/ppermute | solution.py:451
  8.3 8.2 %copy-start = (s32[128]{0:T(128)S(1)}, s32[128]{0:T(128)}, u32[]{:S(2)}) copy-start(s32[128]{0:T(128)} %live_rows.3) | copy-start | bytes 1540
  8.3 8.2 %copy-start.1 = (s32[128]{0:T(128)S(1)}, s32[128]{0:T(128)}, u32[]{:S(2)}) copy-start(s32[128]{0:T(128)} %live_cols.3) | copy-start | bytes 1540
  33.1 13.1 %collective-permute-start.2 = (bf16[112,2048]{1,0:T(8,128)(2,1)S(1)}, bf16[112,2048]{1,0:T(8,128)(2,1)S(1)}, u32[]{:S(2)}, u32[]{:S(2)}) collective-permute-start(bf16[112,2048]{1,0:T(8,128)(2,1)S(1)} %get-tuple-element.47), channel_id=1, source_target_pairs={{0,1},{1,0},{2,3},{3,2},{4,5},{5,4},{6,7},{7,6},{8,9},{9,8},{10,11... | collective-permute-start | bytes 1376264 | tf_op jit(solution)/shard_map/ppermute | solution.py:493
  33.2 9.7 %collective-permute-start.3 = (bf16[112,1024]{1,0:T(8,128)(2,1)S(1)}, bf16[112,1024]{1,0:T(8,128)(2,1)S(1)}, u32[]{:S(2)}, u32[]{:S(2)}) collective-permute-start(bf16[112,1024]{1,0:T(8,128)(2,1)S(1)} %get-tuple-element.48), channel_id=1, source_target_pairs={{0,15},{1,2},{2,1},{3,4},{4,3},{5,6},{6,5},{7,8},{8,7},{9,10},{10,... | collective-permute-start | bytes 688136 | tf_op jit(solution)/shard_map/ppermute | solution.py:486
  35.0 11.2 %collective-permute-start.4 = (bf16[112,1024]{1,0:T(8,128)(2,1)S(1)}, bf16[112,1024]{1,0:T(8,128)(2,1)S(1)}, u32[]{:S(2)}, u32[]{:S(2)}) collective-permute-start(bf16[112,1024]{1,0:T(8,128)(2,1)S(1)} %get-tuple-element.49), channel_id=1, source_target_pairs={{0,15},{1,2},{2,1},{3,4},{4,3},{5,6},{6,5},{7,8},{8,7},{9,10},{10,... | collective-permute-start | bytes 688136 | tf_op jit(solution)/shard_map/ppermute | solution.py:492
